TPU v7x, 32 devices: a whole 2x2x4 slice. The times are simulated.
32 devices in a mesh: chan: 8 (over y, x, core), space: 4 (over z).
Axes of the slice: x: 2, y: 2, z: 4, core: 2. Of those that a mesh axis runs over, the one named last changes fastest.
Arguments:
- u_rows: int32 [64, 8192], P('chan', 'space'), may hold values from 0 to 8191, as said below
- v_cols: int32 [64, 8192], P('chan', 'space'), may hold values from 0 to 8191
- weights: float32 [64, 8192], P('chan', 'space'), may hold values from 0.1 to 10
- tau: float32 [64], P('chan'), may hold values from -0.75 to 0.75
- crop_start: int32 [2], replicated, may hold values from 0 to 8064
Outputs:
- psf: float32 [5, 128, 128], replicated
Inputs may be any that keep to these rules, and one draw needn't show every extreme that they name: u_rows[c, j] lies in row tile j // 2048: from (j // 2048) * 2048 to (j // 2048 + 1) * 2048 - 1.
All inputs are finite; a program needn't handle non-finite values.
Results may differ from a plain program's by a relative error of at most 0.0032.
Values sent between devices are 32-bit elements; how exact they have to be, the bound alone decides.
No kernel may reach another device: no remote copies, remote signals or barrier semaphores. Data moves between devices by JAX's collectives and lax.ppermute only.
A program may use at most 128 MiB of HBM per device.

v0:
```python
import math

import jax
import jax.numpy as jnp
from jax import lax
from jax.sharding import PartitionSpec as P

G = 8192
P_SIZE = 128
TERMS = 5


def col_tables(columns_in, weight_row, crop_start):
    columns = crop_start[1] + jnp.arange(P_SIZE, dtype=jnp.int32)
    phases = columns_in[..., None] * columns % G
    angles = phases.astype(jnp.float32) * (2.0 * math.pi / G)
    scaled = weight_row[..., None]
    return jnp.concatenate([scaled * jnp.cos(angles), scaled * jnp.sin(angles)], axis=-1).astype(
        jnp.bfloat16
    )


def taylor_powers(tau):
    terms_list = [jnp.ones_like(tau)]
    for degree in range(TERMS - 1):
        terms_list.append(terms_list[-1] * tau)
    return jnp.stack(terms_list, axis=-1)


def row_transform(row_ids, grids, crop_start):
    lines = crop_start[0] + jnp.arange(P_SIZE, dtype=jnp.int32)
    phases = lines[:, None] * row_ids[None, :] % G
    angles = phases.astype(jnp.float32) * (2.0 * math.pi / G)
    flat = grids.reshape(grids.shape[0], TERMS * 2 * P_SIZE)
    cos_part = jnp.dot(
        jnp.cos(angles), flat, precision=lax.Precision.HIGHEST, preferred_element_type=jnp.float32
    ).reshape(P_SIZE, TERMS, 2 * P_SIZE)
    sin_part = jnp.dot(
        jnp.sin(angles), flat, precision=lax.Precision.HIGHEST, preferred_element_type=jnp.float32
    ).reshape(P_SIZE, TERMS, 2 * P_SIZE)
    return jnp.transpose(cos_part[:, :, :P_SIZE] - sin_part[:, :, P_SIZE:], (1, 0, 2))


def on_device(u_rows, v_cols, weights, tau, crop_start):
    tile_rows = G // lax.axis_size("space")
    row_base = lax.axis_index("space") * tile_rows
    positions = jnp.arange(tile_rows, dtype=jnp.int32)
    powers = taylor_powers(tau)

    def add_channel(carry, inputs):
        rows_in, cols_in, weight_row, power = inputs
        tables = col_tables(cols_in, weight_row, crop_start)
        onehot = (positions[:, None] == (rows_in - row_base)[None, :]).astype(jnp.bfloat16)
        grids = jnp.dot(onehot, tables, preferred_element_type=jnp.float32)
        return (carry + power[None, :, None] * grids[:, None, :], None)

    taylor, _ = lax.scan(
        add_channel,
        jnp.zeros((tile_rows, TERMS, 2 * P_SIZE), jnp.float32),
        (u_rows, v_cols, weights, powers),
    )
    share = tile_rows // lax.axis_size("chan")
    flat = taylor.reshape(tile_rows, TERMS * 2 * P_SIZE)
    summed = lax.psum_scatter(flat, "chan", scatter_dimension=0, tiled=True)
    row_ids = row_base + lax.axis_index("chan") * share + jnp.arange(share, dtype=jnp.int32)
    beam_part = row_transform(row_ids, summed.reshape(share, TERMS, 2 * P_SIZE), crop_start)
    squares = jnp.sum(weights * weights)
    beam_sum, square_sum = lax.psum((beam_part, squares), ("chan", "space"))
    return beam_sum / jnp.sqrt(square_sum)


def solution(mesh):
    in_specs = (P("chan", "space"), P("chan", "space"), P("chan", "space"), P("chan"), P())
    out_specs = P()
    return jax.shard_map(
        on_device, mesh=mesh, in_specs=in_specs, out_specs=out_specs, check_vma=False
    )
```

profile of v0, /device:TPU:0, one launch (start us, length us, event | category | flops | bytes accessed | tf_op | source)
XLA Modules:
  0.0 439.6 jit_solution(13680139465308641159)
XLA Ops:
  8.0 189.1 %while.13 = (s32[]{:T(128)}, f32[2048,5,256]{2,1,0:T(8,128)}, f32[8,5]{1,0:T(8,128)S(1)}, s32[8,2048]{1,0:T(8,128)}, s32[]{:T(128)}, /*index=5*/f32[8,2048]{1,0:...) while((s32[]{:T(128)}, f32[2048,5,256]{2,1,0:T(8,128)}, f32[8,5]{1,0:T(8,128)S(1)}, ...), condition=%wide.region_1.2_spmd.clone, body=%wide.region_0.1_spmd.clone.sunk | while | flops 2166360320 | bytes 27337924 | solution.py:57
  8.0 0.9 dynamic-slice_subtract_fusion.2
  8.8 0.9 constant_dynamic-slice_fusion.4
  9.7 1.3 slice.26
  11.0 0.7 iota_add_fusion.4
  11.7 5.5 %multiply_convert_fusion.3 = (bf16[2048,128]{1,0:T(8,128)(2,1)S(1)}, bf16[2048,128]{1,0:T(8,128)(2,1)S(1)}) fusion(s32[128]{0:T(128)S(1)} %iota_add_fusion.4, s32[2048]{0:T(1024)S(1)} %bitcast.36, f32[2048]{0:T(1024)S(1)} %bitcast.35), kind=kLoop, calls=%fused_computation.17.clone.1 | loop fusion | flops 4718592 | bytes 1065472 | tf_op jit(solution)/shard_map/convert
  17.2 3.2 fusion.37
  20.4 6.8 %select_add_fusion.2 = f32[2048,5,256]{2,1,0:T(8,128)} fusion(f32[2048,5,256]{2,1,0:T(8,128)} %get-tuple-element.256, f32[2048,256]{1,0:T(8,128)S(1)} %fusion.37, f32[5]{0:T(128)S(1)} %fusion.38, pred[]{:T(512)S(6)} %compare.5), kind=kLoop, calls=%fused_computation.2.clone.1 | loop fusion | flops 7864320 | bytes 23068692 | tf_op jit(solution)/shard_map/while/body/eval_jaxpr/add | solution.py:55
  27.2 0.9 dynamic-slice_subtract_fusion.2
  28.1 0.9 constant_dynamic-slice_fusion.4
  28.9 1.3 slice.26
  30.2 0.7 iota_add_fusion.4
  30.9 5.5 %multiply_convert_fusion.3 = (bf16[2048,128]{1,0:T(8,128)(2,1)S(1)}, bf16[2048,128]{1,0:T(8,128)(2,1)S(1)}) fusion(s32[128]{0:T(128)S(1)} %iota_add_fusion.4, s32[2048]{0:T(1024)S(1)} %bitcast.36, f32[2048]{0:T(1024)S(1)} %bitcast.35), kind=kLoop, calls=%fused_computation.17.clone.1 | loop fusion | flops 4718592 | bytes 1065472 | tf_op jit(solution)/shard_map/convert
  36.4 3.2 fusion.37
  39.6 11.8 %select_add_fusion.2 = f32[2048,5,256]{2,1,0:T(8,128)} fusion(f32[2048,5,256]{2,1,0:T(8,128)} %get-tuple-element.256, f32[2048,256]{1,0:T(8,128)S(1)} %fusion.37, f32[5]{0:T(128)S(1)} %fusion.38, pred[]{:T(512)S(6)} %compare.5), kind=kLoop, calls=%fused_computation.2.clone.1 | loop fusion | flops 7864320 | bytes 23068692 | tf_op jit(solution)/shard_map/while/body/eval_jaxpr/add | solution.py:55
  51.4 0.9 dynamic-slice_subtract_fusion.2
  52.3 0.9 constant_dynamic-slice_fusion.4
  53.2 1.3 slice.26
  54.5 0.7 iota_add_fusion.4
  55.2 5.5 %multiply_convert_fusion.3 = (bf16[2048,128]{1,0:T(8,128)(2,1)S(1)}, bf16[2048,128]{1,0:T(8,128)(2,1)S(1)}) fusion(s32[128]{0:T(128)S(1)} %iota_add_fusion.4, s32[2048]{0:T(1024)S(1)} %bitcast.36, f32[2048]{0:T(1024)S(1)} %bitcast.35), kind=kLoop, calls=%fused_computation.17.clone.1 | loop fusion | flops 4718592 | bytes 1065472 | tf_op jit(solution)/shard_map/convert
  60.7 3.2 fusion.37
  63.9 11.8 %select_add_fusion.2 = f32[2048,5,256]{2,1,0:T(8,128)} fusion(f32[2048,5,256]{2,1,0:T(8,128)} %get-tuple-element.256, f32[2048,256]{1,0:T(8,128)S(1)} %fusion.37, f32[5]{0:T(128)S(1)} %fusion.38, pred[]{:T(512)S(6)} %compare.5), kind=kLoop, calls=%fused_computation.2.clone.1 | loop fusion | flops 7864320 | bytes 23068692 | tf_op jit(solution)/shard_map/while/body/eval_jaxpr/add | solution.py:55
  75.7 0.9 dynamic-slice_subtract_fusion.2
  76.6 0.9 constant_dynamic-slice_fusion.4
  77.5 1.3 slice.26
  78.8 0.7 iota_add_fusion.4
  79.5 5.5 %multiply_convert_fusion.3 = (bf16[2048,128]{1,0:T(8,128)(2,1)S(1)}, bf16[2048,128]{1,0:T(8,128)(2,1)S(1)}) fusion(s32[128]{0:T(128)S(1)} %iota_add_fusion.4, s32[2048]{0:T(1024)S(1)} %bitcast.36, f32[2048]{0:T(1024)S(1)} %bitcast.35), kind=kLoop, calls=%fused_computation.17.clone.1 | loop fusion | flops 4718592 | bytes 1065472 | tf_op jit(solution)/shard_map/convert
  84.9 3.2 fusion.37
  88.1 11.8 %select_add_fusion.2 = f32[2048,5,256]{2,1,0:T(8,128)} fusion(f32[2048,5,256]{2,1,0:T(8,128)} %get-tuple-element.256, f32[2048,256]{1,0:T(8,128)S(1)} %fusion.37, f32[5]{0:T(128)S(1)} %fusion.38, pred[]{:T(512)S(6)} %compare.5), kind=kLoop, calls=%fused_computation.2.clone.1 | loop fusion | flops 7864320 | bytes 23068692 | tf_op jit(solution)/shard_map/while/body/eval_jaxpr/add | solution.py:55
  100.0 0.9 dynamic-slice_subtract_fusion.2
  100.9 0.9 constant_dynamic-slice_fusion.4
  101.7 1.3 slice.26
  103.0 0.7 iota_add_fusion.4
  103.7 5.5 %multiply_convert_fusion.3 = (bf16[2048,128]{1,0:T(8,128)(2,1)S(1)}, bf16[2048,128]{1,0:T(8,128)(2,1)S(1)}) fusion(s32[128]{0:T(128)S(1)} %iota_add_fusion.4, s32[2048]{0:T(1024)S(1)} %bitcast.36, f32[2048]{0:T(1024)S(1)} %bitcast.35), kind=kLoop, calls=%fused_computation.17.clone.1 | loop fusion | flops 4718592 | bytes 1065472 | tf_op jit(solution)/shard_map/convert
  109.2 3.2 fusion.37
  112.4 11.8 %select_add_fusion.2 = f32[2048,5,256]{2,1,0:T(8,128)} fusion(f32[2048,5,256]{2,1,0:T(8,128)} %get-tuple-element.256, f32[2048,256]{1,0:T(8,128)S(1)} %fusion.37, f32[5]{0:T(128)S(1)} %fusion.38, pred[]{:T(512)S(6)} %compare.5), kind=kLoop, calls=%fused_computation.2.clone.1 | loop fusion | flops 7864320 | bytes 23068692 | tf_op jit(solution)/shard_map/while/body/eval_jaxpr/add | solution.py:55
  124.2 0.9 dynamic-slice_subtract_fusion.2
  125.1 0.9 constant_dynamic-slice_fusion.4
  126.0 1.3 slice.26
  127.3 0.7 iota_add_fusion.4
  128.0 5.5 %multiply_convert_fusion.3 = (bf16[2048,128]{1,0:T(8,128)(2,1)S(1)}, bf16[2048,128]{1,0:T(8,128)(2,1)S(1)}) fusion(s32[128]{0:T(128)S(1)} %iota_add_fusion.4, s32[2048]{0:T(1024)S(1)} %bitcast.36, f32[2048]{0:T(1024)S(1)} %bitcast.35), kind=kLoop, calls=%fused_computation.17.clone.1 | loop fusion | flops 4718592 | bytes 1065472 | tf_op jit(solution)/shard_map/convert
  133.5 3.2 fusion.37
  136.7 11.8 %select_add_fusion.2 = f32[2048,5,256]{2,1,0:T(8,128)} fusion(f32[2048,5,256]{2,1,0:T(8,128)} %get-tuple-element.256, f32[2048,256]{1,0:T(8,128)S(1)} %fusion.37, f32[5]{0:T(128)S(1)} %fusion.38, pred[]{:T(512)S(6)} %compare.5), kind=kLoop, calls=%fused_computation.2.clone.1 | loop fusion | flops 7864320 | bytes 23068692 | tf_op jit(solution)/shard_map/while/body/eval_jaxpr/add | solution.py:55
  148.5 0.9 dynamic-slice_subtract_fusion.2
  149.4 0.9 constant_dynamic-slice_fusion.4
  150.2 1.3 slice.26
  152.3 5.5 %multiply_convert_fusion.3 = (bf16[2048,128]{1,0:T(8,128)(2,1)S(1)}, bf16[2048,128]{1,0:T(8,128)(2,1)S(1)}) fusion(s32[128]{0:T(128)S(1)} %iota_add_fusion.4, s32[2048]{0:T(1024)S(1)} %bitcast.36, f32[2048]{0:T(1024)S(1)} %bitcast.35), kind=kLoop, calls=%fused_computation.17.clone.1 | loop fusion | flops 4718592 | bytes 1065472 | tf_op jit(solution)/shard_map/convert
  157.7 3.2 fusion.37
  160.9 11.8 %select_add_fusion.2 = f32[2048,5,256]{2,1,0:T(8,128)} fusion(f32[2048,5,256]{2,1,0:T(8,128)} %get-tuple-element.256, f32[2048,256]{1,0:T(8,128)S(1)} %fusion.37, f32[5]{0:T(128)S(1)} %fusion.38, pred[]{:T(512)S(6)} %compare.5), kind=kLoop, calls=%fused_computation.2.clone.1 | loop fusion | flops 7864320 | bytes 23068692 | tf_op jit(solution)/shard_map/while/body/eval_jaxpr/add | solution.py:55
  172.8 0.9 dynamic-slice_subtract_fusion.2
  173.7 0.9 constant_dynamic-slice_fusion.4
  174.5 1.3 slice.26
  176.5 5.5 %multiply_convert_fusion.3 = (bf16[2048,128]{1,0:T(8,128)(2,1)S(1)}, bf16[2048,128]{1,0:T(8,128)(2,1)S(1)}) fusion(s32[128]{0:T(128)S(1)} %iota_add_fusion.4, s32[2048]{0:T(1024)S(1)} %bitcast.36, f32[2048]{0:T(1024)S(1)} %bitcast.35), kind=kLoop, calls=%fused_computation.17.clone.1 | loop fusion | flops 4718592 | bytes 1065472 | tf_op jit(solution)/shard_map/convert
  182.0 3.2 fusion.37
  185.2 11.8 %select_add_fusion.2 = f32[2048,5,256]{2,1,0:T(8,128)} fusion(f32[2048,5,256]{2,1,0:T(8,128)} %get-tuple-element.256, f32[2048,256]{1,0:T(8,128)S(1)} %fusion.37, f32[5]{0:T(128)S(1)} %fusion.38, pred[]{:T(512)S(6)} %compare.5), kind=kLoop, calls=%fused_computation.2.clone.1 | loop fusion | flops 7864320 | bytes 23068692 | tf_op jit(solution)/shard_map/while/body/eval_jaxpr/add | solution.py:55
  197.0 15.1 %copy.10 = f32[2048,5,256]{0,2,1:T(8,128)} copy(f32[2048,5,256]{2,1,0:T(8,128)} %get-tuple-element.119) | data formatting | bytes 20971520 | tf_op jit(solution)/shard_map/while | solution.py:57
  212.9 83.9 %reduce-scatter.2.cloned.1.call-done = f32[256,1280]{0,1:T(8,128)} async-done(((f32[2048,1280]{0,1:T(8,128)}), f32[256,1280]{0,1:T(8,128)}) %reduce-scatter.2.cloned.1.call-update) | async-done | bytes 1310736 | tf_op jit(solution)/shard_map/reduce_scatter | solution.py:64
  296.7 3.1 fusion.18
  299.8 3.1 fusion.16
  302.9 0.8 fusion.12
  304.3 39.5 %psum.15 = f32[]{:T(128)} all-reduce(f32[]{:T(128)} %multiply_reduce_fusion), channel_id=1, replica_groups=mesh['chan'=8,'space'=4] {'chan','space'}, use_global_device_ids=true, to_apply=%region_5.6 | all-reduce | flops 1 | bytes 8 | tf_op jit(solution)/shard_map/psum | solution.py:68
  344.4 86.5 %all-reduce.2.cloned.1.call-done = f32[5,128,128]{1,2,0:T(8,128)} async-done(((f32[5,128,128]{1,2,0:T(8,128)}), f32[5,128,128]{1,2,0:T(8,128)}) %all-reduce.2.cloned.1.call-update) | async-done | bytes 327696 | tf_op jit(solution)/shard_map/psum | solution.py:68
  430.9 1.0 broadcast_divide_fusion
  431.9 0.9 copy.13
  (26 shorter events, 4.2 us)
Async XLA Ops:
  6.5 290.2 %reduce-scatter.2.cloned.1.call-start = ((), (), s32[]{:S(2)}) async-start(), calls=%async_computation.1 | async-start | bytes 11796480 | tf_op jit(solution)/shard_map/reduce_scatter | solution.py:64
  212.2 0.7 copy-start.1
  212.2 91.5 %copy-start = (f32[8,2048]{1,0:T(8,128)S(1)}, f32[8,2048]{1,0:T(8,128)}, u32[]{:S(2)}) copy-start(f32[8,2048]{1,0:T(8,128)} %get-tuple-element.283) | copy-start | bytes 196612
  212.2 218.7 %all-reduce.2.cloned.1.call-start = ((), (), s32[]{:S(2)}) async-start(), calls=%async_computation.2 | async-start | bytes 655360 | tf_op jit(solution)/shard_map/psum | solution.py:68
Sparse Core Ops, SparseCore 0:
  212.3 84.3 reduce-scatter.1
  303.8 127.0 all-reduce.1
where the time goes:
time: 442 us; the launch traced here: 440 us
  waiting for transfers between devices  170 us (38%)
  other arithmetic  149 us (34%)
  blocking collectives  39.5 us (9%)
  local copies, waits for them, and re-layouts  34.8 us (8%)
  matrix products  31.4 us (7%)
  between operations  14.1 us (3%)
    add x8, other arithmetic, add_channel(): return (carry + power[None, :, None] * grids[:, None, :], None)  89.7 us
    psum x1, waiting for transfers between devices, on_device(): beam_sum, square_sum = lax.psum((beam_part, squares), ('chan', 'space'))  86.5 us
    reduce_scatter x1, waiting for transfers between devices, on_device(): summed = lax.psum_scatter(flat, 'chan', scatter_dimension=0, tiled=True)  83.9 us
    another operation x8, other arithmetic  43.7 us
    psum x1, blocking collectives, on_device(): beam_sum, square_sum = lax.psum((beam_part, squares), ('chan', 'space'))  39.5 us
    dot_general x8, matrix products, add_channel(): grids = jnp.dot(onehot, tables, preferred_element_type=jnp.float32)  25.3 us
    while x1, local copies, waits for them, and re-layouts, on_device(): lax.scan(add_channel, jnp.zeros((tile_rows, TERMS, 2 * P_SIZE), jnp.float...  15.1 us
    slice x8, local copies, waits for them, and re-layouts, col_tables(): columns = crop_start[1] + jnp.arange(P_SIZE, dtype=jnp.int32)  10.5 us
  transfers between devices with their start and end apart: 2, of which 2 were waited for; matrix products, arithmetic and copies ran while one was open for 0% of the time, Pallas kernels for 0%

commit v1 on v0

v1 whole, which is shorter than its diff:
```python
import functools
import math

import jax
import jax.numpy as jnp
from jax import lax
from jax.experimental import pallas as pl
from jax.experimental.pallas import tpu as pltpu
from jax.sharding import PartitionSpec as P

G = 8192
P_SIZE = 128
TERMS = 5
HALF = P_SIZE // 2
STEP = 8
WIDTH = 256
QUARTER = G // 4


def sin_cos(phase):
    quadrant = (phase + QUARTER // 2) >> (QUARTER.bit_length() - 1)
    rest = phase - quadrant * QUARTER
    x = rest.astype(jnp.float32) * (2.0 * math.pi / G)
    z = x * x
    s = x + x * z * (-1.6666654611e-1 + z * (8.3321608736e-3 + z * -1.9515295891e-4))
    c = 1.0 - 0.5 * z + z * z * (4.166664568298827e-2 + z * (-1.388731625493765e-3 + z * 2.443315711809948e-5))
    odd = (quadrant & 1) == 1
    sin_value = jnp.where(odd, c, s)
    cos_value = jnp.where(odd, s, c)
    sin_value = jnp.where((quadrant & 2) == 2, -sin_value, sin_value)
    cos_value = jnp.where(((quadrant + 1) & 2) == 2, -cos_value, cos_value)
    return cos_value, sin_value


def fill_table(table, chunk, ids, start, cos_step, sin_step, scale):
    width = ids.shape[1]
    row = lax.broadcasted_iota(jnp.int32, (STEP, width), 0)
    ids = jnp.broadcast_to(ids, (STEP, width))
    cos_prev, sin_prev = sin_cos((ids * (row + start)) & (G - 1))
    if scale is not None:
        scale = jnp.broadcast_to(scale, (STEP, width))
        cos_prev, sin_prev = cos_prev * scale, sin_prev * scale
    cos_step = jnp.broadcast_to(cos_step, (STEP, width))
    sin_step = jnp.broadcast_to(sin_step, (STEP, width))
    cos_now = cos_prev * cos_step - sin_prev * sin_step
    sin_now = sin_prev * cos_step + cos_prev * sin_step
    twice = cos_step + cos_step
    for first in range(0, P_SIZE, 2 * STEP):
        table[first : first + 2 * STEP, chunk] = jnp.concatenate([cos_prev, cos_now], axis=0).astype(jnp.bfloat16)
        table[P_SIZE + first : P_SIZE + first + 2 * STEP, chunk] = jnp.concatenate(
            [sin_prev, sin_now], axis=0
        ).astype(jnp.bfloat16)
        if first + 2 * STEP < P_SIZE:
            cos_prev = twice * cos_now - cos_prev
            sin_prev = twice * sin_now - sin_prev
            cos_now = twice * cos_prev - cos_now
            sin_now = twice * sin_prev - sin_now


def kernel(
    place_ref, tau_ref, u_ref, v_ref, w_ref, mine_ref, other_ref, row_tables, col_tables, steps, beams
):
    channels, count = u_ref.shape
    row_start, col_start, core = place_ref[0], place_ref[1], place_ref[2]
    for k, ref in enumerate((u_ref, v_ref)):
        cos_step, sin_step = sin_cos((ref[...] * STEP) & (G - 1))
        steps[2 * k], steps[2 * k + 1] = cos_step, sin_step
    beams[...] = jnp.zeros_like(beams)

    def fill(channel, slot):
        one = slice(channel, channel + 1)
        for begin in range(0, count, WIDTH):
            chunk = slice(begin, begin + WIDTH)
            fill_table(
                row_tables.at[slot], chunk, u_ref[one, chunk], row_start, steps[0, one, chunk], steps[1, one, chunk], None
            )
            fill_table(
                col_tables.at[slot],
                chunk,
                v_ref[one, chunk],
                col_start,
                steps[2, one, chunk],
                steps[3, one, chunk],
                w_ref[one, chunk],
            )

    def add(channel, slot):
        product = lax.dot_general(
            row_tables[slot], col_tables[slot], (((1,), (1,)), ((), ())), preferred_element_type=jnp.float32
        )
        beam = product[:P_SIZE, :P_SIZE] - product[P_SIZE:, P_SIZE:]
        tau = tau_ref[channel]
        power = jnp.float32(1.0)
        for term in range(TERMS):
            beams[term] += power * beam
            power = power * tau

    fill(0, 0)
    for channel in range(channels):
        if channel + 1 < channels:
            fill(channel + 1, (channel + 1) % 2)
        add(channel, channel % 2)

    squares = jnp.zeros((channels, P_SIZE), jnp.float32)
    for begin in range(0, count, P_SIZE):
        w = w_ref[:, begin : begin + P_SIZE]
        squares += w * w

    def put(low, high):
        for ref, first in ((low, 0), (high, HALF)):
            for term in range(TERMS):
                ref[term * HALF : (term + 1) * HALF, :] = beams[term, first : first + HALF, :]
            ref[TERMS * HALF :, :] = squares

    pl.when(core == 0)(lambda: put(mine_ref, other_ref))
    pl.when(core == 1)(lambda: put(other_ref, mine_ref))


def partial_beams(u_rows, v_cols, weights, tau, place):
    channels, count = u_rows.shape
    rows = TERMS * HALF + channels
    part = jax.ShapeDtypeStruct((rows, P_SIZE), jnp.float32)
    vmem = pl.BlockSpec(memory_space=pltpu.VMEM)
    smem = pl.BlockSpec(memory_space=pltpu.SMEM)
    return pl.pallas_call(
        kernel,
        out_shape=(part, part),
        in_specs=[smem, smem, vmem, vmem, vmem],
        out_specs=(vmem, vmem),
        scratch_shapes=[
            pltpu.VMEM((2, 2 * P_SIZE, count), jnp.bfloat16),
            pltpu.VMEM((2, 2 * P_SIZE, count), jnp.bfloat16),
            pltpu.VMEM((4, channels, count), jnp.float32),
            pltpu.VMEM((TERMS, P_SIZE, P_SIZE), jnp.float32),
        ],
    )(place, tau, u_rows, v_cols, weights)


def exchange_orders(chan, space):
    over_chan = [("chan", 1 << b) for b in range(1, chan.bit_length() - 1)]
    over_space = [("space", 1 << b) for b in range(space.bit_length() - 1)]
    first = []
    for k in range(max(len(over_chan), len(over_space))):
        first += over_chan[k : k + 1] + over_space[k : k + 1]
    second = list(first)
    for k in range(0, len(second) - 1, 2):
        second[k], second[k + 1] = second[k + 1], second[k]
    return first, second


def on_device(u_rows, v_cols, weights, tau, crop_start):
    chan, space = lax.axis_size("chan"), lax.axis_size("space")
    core = lax.axis_index("chan") % 2
    place = jnp.concatenate([crop_start, core[None]])
    mine, other = partial_beams(u_rows, v_cols, weights, tau, place)
    partner = [(i, i ^ 1) for i in range(chan)]
    total = mine + lax.ppermute(other, "chan", partner)
    for moves in zip(*exchange_orders(chan, space)):
        pairs = []
        for c in range(chan):
            axis, bit = moves[c % 2]
            for s in range(space):
                to = (c ^ bit, s) if axis == "chan" else (c, s ^ bit)
                pairs.append((c * space + s, to[0] * space + to[1]))
        total = total + lax.ppermute(total, ("chan", "space"), pairs)
    beam = total[: TERMS * HALF] / jnp.sqrt(jnp.sum(total[TERMS * HALF :]))
    away = lax.ppermute(beam, "chan", partner)
    low = jnp.where(core == 0, beam, away).reshape(TERMS, HALF, P_SIZE)
    high = jnp.where(core == 0, away, beam).reshape(TERMS, HALF, P_SIZE)
    return jnp.concatenate([low, high], axis=1)


def solution(mesh):
    in_specs = (P("chan", "space"), P("chan", "space"), P("chan", "space"), P("chan"), P())
    return jax.shard_map(on_device, mesh=mesh, in_specs=in_specs, out_specs=P(), check_vma=False)
```

time: 442 us -> 39.9 us (0.09)
  waiting for transfers between devices: 170 us -> 17.8 us
  other arithmetic: 149 us -> 3.09 us
  blocking collectives: 39.5 us -> 0 us
  local copies, waits for them, and re-layouts: 34.8 us -> 0.65 us
  matrix products: 31.4 us -> 0 us
  between operations: 14.1 us -> 0.73 us
  starting transfers between devices: 0.04 us -> 10.8 us
  Pallas kernels: 0 us -> 6.61 us
    add x18 -> x5, other arithmetic: 95.2 us -> 1.03 us  [the longest x1 0.94 us: on_device(): total = mine + lax.ppermute(other, 'chan', partner)]
    psum x1 -> x0, waiting for transfers between devices: 86.5 us -> none  [on_device(): beam_sum, square_sum = lax.psum((beam_part, squares), ('chan', 'space'))]
    reduce_scatter x1 -> x0, waiting for transfers between devices: 83.9 us -> none  [on_device(): summed = lax.psum_scatter(flat, 'chan', scatter_dimension=0, tiled=True)]
    another operation x9 -> x0, other arithmetic: 44.4 us -> none
    psum x1 -> x0, blocking collectives: 39.5 us -> none  [on_device(): beam_sum, square_sum = lax.psum((beam_part, squares), ('chan', 'space'))]
    dot_general x10 -> x0, matrix products: 31.4 us -> none  [the longest x8 25.3 us: add_channel(): grids = jnp.dot(onehot, tables, preferred_element_type=jnp.float32)]
    ppermute x0 -> x6, waiting for transfers between devices: none -> 17.8 us  [the longest x4 15.2 us: on_device(): total = total + lax.ppermute(total, ('chan', 'space'), pairs)]
    while x1 -> x0, local copies, waits for them, and re-layouts: 15.1 us -> none  [on_device(): lax.scan(add_channel, jnp.zeros((tile_rows, TERMS, 2 * P_SIZE), jnp.float...]
  transfers between devices with their start and end apart: 2 -> 6, of which waited for: 2 -> 6; matrix products, arithmetic and copies ran while one was open for 0% -> 0% of each run, Pallas kernels for 0% -> 0%
where the time goes in v1:
time: 39.9 us; the launch traced here: 39.7 us
  waiting for transfers between devices  17.8 us (45%)
  starting transfers between devices  10.8 us (27%)
  Pallas kernels  6.61 us (17%)
  other arithmetic  3.09 us (8%)
  between operations  0.73 us (2%)
  local copies, waits for them, and re-layouts  0.65 us (2%)
    ppermute x4, waiting for transfers between devices, on_device(): total = total + lax.ppermute(total, ('chan', 'space'), pairs)  15.2 us
    ppermute x4, starting transfers between devices, on_device(): total = total + lax.ppermute(total, ('chan', 'space'), pairs)  10.2 us
    pallas_call x1, Pallas kernels, partial_beams(): pl.pallas_call(kernel, out_shape=(part, part), in_specs=[smem, smem, vmem...  6.61 us
    ppermute x1, waiting for transfers between devices, on_device(): away = lax.ppermute(beam, 'chan', partner)  1.38 us
    ppermute x1, waiting for transfers between devices, on_device(): total = mine + lax.ppermute(other, 'chan', partner)  1.24 us
    add x1, other arithmetic, on_device(): total = mine + lax.ppermute(other, 'chan', partner)  0.94 us
  transfers between devices with their start and end apart: 6, of which 6 were waited for; matrix products, arithmetic and copies ran while one was open for 0% of the time, Pallas kernels for 0%

profile of v1, /device:TPU:0, one launch (start us, length us, event | category | flops | bytes accessed | tf_op | source)
XLA Modules:
  0.0 39.7 jit_solution(14492081451079656929)
XLA Ops:
  0.0 0.0 copy-start
  0.0 0.7 %copy-done = s32[2]{0:T(128)S(1)} copy-done((s32[2]{0:T(128)S(1)}, s32[2]{0:T(128)}, u32[]{:S(2)}) %copy-start) | copy-done | bytes 32
  0.7 0.7 %pad_add_fusion.place_ref = s32[3]{0:T(128)} fusion(s32[1]{0:T(128)} %bitcast, s32[2]{0:T(128)S(1)} %copy-done), kind=kLoop, calls=%fused_computation.5 | loop fusion | flops 3 | bytes 24 | tf_op jit(solution)/shard_map/concatenate | solution.py:154
  1.3 6.6 %shard_map.55 = (f32[328,128]{1,0:T(8,128)}, f32[328,128]{1,0:T(8,128)}) custom-call(s32[3]{0:T(128)} %pad_add_fusion.place_ref, f32[8]{0:T(128)} %tau_ref.1, s32[8,2048]{1,0:T(8,128)} %u_ref.1, s32[8,2048]{1,0:T(8,128)} %v_ref.1, f32[8,2048]{1,0:T(8,128)} %w_ref.1), custom_call_target="tpu_custom_call" | custom-call | tf_op jit(solution)/shard_map/pallas_call | solution.py:125
  7.9 0.5 %collective-permute-start = (f32[328,128]{1,0:T(8,128)}, f32[328,128]{1,0:T(8,128)S(1)}, u32[]{:S(2)}, u32[]{:S(2)}) collective-permute-start(f32[328,128]{1,0:T(8,128)} %get-tuple-element.8), channel_id=1, source_target_pairs={{0,4},{4,0},{8,12},{12,8},{16,20},{20,16},{24,28},{28,24},{1,5},{5... | collective-permute-start | bytes 503816 | tf_op jit(solution)/shard_map/ppermute | solution.py:157
  8.4 1.2 %collective-permute-done = f32[328,128]{1,0:T(8,128)S(1)} collective-permute-done((f32[328,128]{1,0:T(8,128)}, f32[328,128]{1,0:T(8,128)S(1)}, u32[]{:S(2)}, u32[]{:S(2)}) %collective-permute-start) | collective-permute-done | bytes 167968 | tf_op jit(solution)/shard_map/ppermute | solution.py:157
  9.7 0.9 %add.20 = f32[328,128]{1,0:T(8,128)S(1)} add(f32[328,128]{1,0:T(8,128)} %get-tuple-element.7, f32[328,128]{1,0:T(8,128)S(1)} %collective-permute-done) | non-fusion elementwise | flops 41984 | bytes 503808 | tf_op jit(solution)/shard_map/add | solution.py:157
  10.6 2.9 %collective-permute-start.1 = (f32[328,128]{1,0:T(8,128)S(1)}, f32[328,128]{1,0:T(8,128)S(1)}, u32[]{:S(2)}, u32[]{:S(2)}) collective-permute-start(f32[328,128]{1,0:T(8,128)S(1)} %add.20), channel_id=1, source_target_pairs={{0,8},{1,9},{2,10},{3,11},{4,5},{5,4},{6,7},{7,6},{8,0},{9,1},{10,... | collective-permute-start | bytes 503816 | tf_op jit(solution)/shard_map/ppermute | solution.py:165
  13.5 3.3 %collective-permute-done.1 = f32[328,128]{1,0:T(8,128)S(1)} collective-permute-done((f32[328,128]{1,0:T(8,128)S(1)}, f32[328,128]{1,0:T(8,128)S(1)}, u32[]{:S(2)}, u32[]{:S(2)}) %collective-permute-start.1) | collective-permute-done | bytes 167968 | tf_op jit(solution)/shard_map/ppermute | solution.py:165
  16.9 2.2 %collective-permute-start.2 = (f32[328,128]{1,0:T(8,128)S(1)}, f32[328,128]{1,0:T(8,128)S(1)}, u32[]{:S(2)}, u32[]{:S(2)}) collective-permute-start(f32[328,128]{1,0:T(8,128)S(1)} %add.21), channel_id=1, source_target_pairs={{0,1},{1,0},{2,3},{3,2},{4,12},{5,13},{6,14},{7,15},{8,9},{9,8},{1... | collective-permute-start | bytes 503816 | tf_op jit(solution)/shard_map/ppermute | solution.py:165
  19.1 3.3 %collective-permute-done.2 = f32[328,128]{1,0:T(8,128)S(1)} collective-permute-done((f32[328,128]{1,0:T(8,128)S(1)}, f32[328,128]{1,0:T(8,128)S(1)}, u32[]{:S(2)}, u32[]{:S(2)}) %collective-permute-start.2) | collective-permute-done | bytes 167968 | tf_op jit(solution)/shard_map/ppermute | solution.py:165
  22.4 2.0 %collective-permute-start.3 = (f32[328,128]{1,0:T(8,128)S(1)}, f32[328,128]{1,0:T(8,128)S(1)}, u32[]{:S(2)}, u32[]{:S(2)}) collective-permute-start(f32[328,128]{1,0:T(8,128)S(1)} %add.22), channel_id=1, source_target_pairs={{0,16},{1,17},{2,18},{3,19},{4,6},{5,7},{6,4},{7,5},{8,24},{9,25},... | collective-permute-start | bytes 503816 | tf_op jit(solution)/shard_map/ppermute | solution.py:165
  24.5 3.4 %collective-permute-done.3 = f32[328,128]{1,0:T(8,128)S(1)} collective-permute-done((f32[328,128]{1,0:T(8,128)S(1)}, f32[328,128]{1,0:T(8,128)S(1)}, u32[]{:S(2)}, u32[]{:S(2)}) %collective-permute-start.3) | collective-permute-done | bytes 167968 | tf_op jit(solution)/shard_map/ppermute | solution.py:165
  27.9 3.1 %collective-permute-start.4 = (f32[328,128]{1,0:T(8,128)S(1)}, f32[328,128]{1,0:T(8,128)S(1)}, u32[]{:S(2)}, u32[]{:S(2)}) collective-permute-start(f32[328,128]{1,0:T(8,128)S(1)} %add.23), channel_id=1, source_target_pairs={{0,2},{1,3},{2,0},{3,1},{4,20},{5,21},{6,22},{7,23},{8,10},{9,11},... | collective-permute-start | bytes 503816 | tf_op jit(solution)/shard_map/ppermute | solution.py:165
  31.0 5.1 %collective-permute-done.4 = f32[328,128]{1,0:T(8,128)S(1)} collective-permute-done((f32[328,128]{1,0:T(8,128)S(1)}, f32[328,128]{1,0:T(8,128)S(1)}, u32[]{:S(2)}, u32[]{:S(2)}) %collective-permute-start.4) | collective-permute-done | bytes 167968 | tf_op jit(solution)/shard_map/ppermute | solution.py:165
  36.1 0.6 %slice_reduce_fusion = f32[]{:T(128)} fusion(f32[328,128]{1,0:T(8,128)S(1)} %add.24), kind=kLoop, calls=%fused_computation.4 | loop fusion | flops 1023 | bytes 4100 | tf_op jit(solution)/shard_map/reduce_sum | solution.py:166
  37.5 0.1 collective-permute-start.5
  37.5 1.4 %collective-permute-done.5 = f32[320,128]{1,0:T(8,128)S(1)} collective-permute-done((f32[320,128]{1,0:T(8,128)S(1)}, f32[320,128]{1,0:T(8,128)S(1)}, u32[]{:S(2)}, u32[]{:S(2)}) %collective-permute-start.5) | collective-permute-done | bytes 163872 | tf_op jit(solution)/shard_map/ppermute | solution.py:167
  39.0 0.7 %pad_maximum_fusion = f32[5,128,128]{2,1,0:T(8,128)} fusion(f32[5,64,128]{2,1,0:T(8,128)S(1)} %bitcast.4, f32[5,64,128]{2,1,0:T(8,128)S(1)} %bitcast.3), kind=kLoop, calls=%fused_computation | loop fusion | flops 81920 | bytes 655360 | tf_op jit(solution)/shard_map/concatenate | solution.py:170
  (6 shorter events, 0.1 us)
Async XLA Ops:
  0.0 0.7 %copy-start = (s32[2]{0:T(128)S(1)}, s32[2]{0:T(128)}, u32[]{:S(2)}) copy-start(s32[2]{0:T(128)} %param.9) | copy-start | bytes 28
  7.9 1.7 %collective-permute-start = (f32[328,128]{1,0:T(8,128)}, f32[328,128]{1,0:T(8,128)S(1)}, u32[]{:S(2)}, u32[]{:S(2)}) collective-permute-start(f32[328,128]{1,0:T(8,128)} %get-tuple-element.8), channel_id=1, source_target_pairs={{0,4},{4,0},{8,12},{12,8},{16,20},{20,16},{24,28},{28,24},{1,5},{5... | collective-permute-start | bytes 503816 | tf_op jit(solution)/shard_map/ppermute | solution.py:157
  10.6 6.3 %collective-permute-start.1 = (f32[328,128]{1,0:T(8,128)S(1)}, f32[328,128]{1,0:T(8,128)S(1)}, u32[]{:S(2)}, u32[]{:S(2)}) collective-permute-start(f32[328,128]{1,0:T(8,128)S(1)} %add.20), channel_id=1, source_target_pairs={{0,8},{1,9},{2,10},{3,11},{4,5},{5,4},{6,7},{7,6},{8,0},{9,1},{10,... | collective-permute-start | bytes 503816 | tf_op jit(solution)/shard_map/ppermute | solution.py:165
  16.9 5.5 %collective-permute-start.2 = (f32[328,128]{1,0:T(8,128)S(1)}, f32[328,128]{1,0:T(8,128)S(1)}, u32[]{:S(2)}, u32[]{:S(2)}) collective-permute-start(f32[328,128]{1,0:T(8,128)S(1)} %add.21), channel_id=1, source_target_pairs={{0,1},{1,0},{2,3},{3,2},{4,12},{5,13},{6,14},{7,15},{8,9},{9,8},{1... | collective-permute-start | bytes 503816 | tf_op jit(solution)/shard_map/ppermute | solution.py:165
  22.4 5.4 %collective-permute-start.3 = (f32[328,128]{1,0:T(8,128)S(1)}, f32[328,128]{1,0:T(8,128)S(1)}, u32[]{:S(2)}, u32[]{:S(2)}) collective-permute-start(f32[328,128]{1,0:T(8,128)S(1)} %add.22), channel_id=1, source_target_pairs={{0,16},{1,17},{2,18},{3,19},{4,6},{5,7},{6,4},{7,5},{8,24},{9,25},... | collective-permute-start | bytes 503816 | tf_op jit(solution)/shard_map/ppermute | solution.py:165
  27.9 8.2 %collective-permute-start.4 = (f32[328,128]{1,0:T(8,128)S(1)}, f32[328,128]{1,0:T(8,128)S(1)}, u32[]{:S(2)}, u32[]{:S(2)}) collective-permute-start(f32[328,128]{1,0:T(8,128)S(1)} %add.23), channel_id=1, source_target_pairs={{0,2},{1,3},{2,0},{3,1},{4,20},{5,21},{6,22},{7,23},{8,10},{9,11},... | collective-permute-start | bytes 503816 | tf_op jit(solution)/shard_map/ppermute | solution.py:165
  37.5 1.5 %collective-permute-start.5 = (f32[320,128]{1,0:T(8,128)S(1)}, f32[320,128]{1,0:T(8,128)S(1)}, u32[]{:S(2)}, u32[]{:S(2)}) collective-permute-start(f32[320,128]{1,0:T(8,128)S(1)} %slice_divide_fusion), channel_id=1, source_target_pairs={{0,4},{4,0},{8,12},{12,8},{16,20},{20,16},{24,28},{28,24},{1,5},{5... | collective-permute-start | bytes 491528 | tf_op jit(solution)/shard_map/ppermute | solution.py:167

commit v2 on v1

v2 whole, which is shorter than its diff:
```python
import math

import jax
import jax.numpy as jnp
from jax import lax
from jax.experimental import pallas as pl
from jax.experimental.pallas import tpu as pltpu
from jax.sharding import PartitionSpec as P

G = 8192
P_SIZE = 128
TERMS = 5
HALF = P_SIZE // 2
STEP = 8
WIDTH = 128
QUARTER = G // 4


def sin_cos(phase):
    quadrant = (phase + QUARTER // 2) >> (QUARTER.bit_length() - 1)
    rest = phase - quadrant * QUARTER
    x = rest.astype(jnp.float32) * (2.0 * math.pi / G)
    z = x * x
    s = x + x * z * (-1.6666654611e-1 + z * (8.3321608736e-3 + z * -1.9515295891e-4))
    c = 1.0 - 0.5 * z + z * z * (4.166664568298827e-2 + z * (-1.388731625493765e-3 + z * 2.443315711809948e-5))
    odd = (quadrant & 1) == 1
    sin_value = jnp.where(odd, c, s)
    cos_value = jnp.where(odd, s, c)
    sin_value = jnp.where((quadrant & 2) == 2, -sin_value, sin_value)
    cos_value = jnp.where(((quadrant + 1) & 2) == 2, -cos_value, cos_value)
    return cos_value, sin_value


def prepare(ids, start, scale, seeds, steps):
    cos_one, sin_one = sin_cos(ids)
    cos_prev, sin_prev = sin_cos((ids * start) & (G - 1))
    if scale is not None:
        cos_prev, sin_prev = cos_prev * scale, sin_prev * scale
    cos_now = cos_prev * cos_one - sin_prev * sin_one
    sin_now = sin_prev * cos_one + cos_prev * sin_one
    twice = cos_one + cos_one
    channels, count = ids.shape
    for row in range(STEP):
        rows = pl.ds(row, channels, stride=STEP)
        for group in range(count // WIDTH):
            chunk = slice(group * WIDTH, (group + 1) * WIDTH)
            seeds[0, group, rows, :] = cos_prev[:, chunk]
            seeds[1, group, rows, :] = sin_prev[:, chunk]
        cos_prev, cos_now = cos_now, twice * cos_now - cos_prev
        sin_prev, sin_now = sin_now, twice * sin_now - sin_prev
    steps[0], steps[1] = sin_cos((ids * STEP) & (G - 1))


def fill_table(table, chunk, cos_prev, sin_prev, cos_step, sin_step):
    cos_step = jnp.broadcast_to(cos_step, cos_prev.shape)
    sin_step = jnp.broadcast_to(sin_step, cos_prev.shape)
    cos_now = cos_prev * cos_step - sin_prev * sin_step
    sin_now = sin_prev * cos_step + cos_prev * sin_step
    twice = cos_step + cos_step
    for first in range(0, P_SIZE, 2 * STEP):
        table[first : first + 2 * STEP, chunk] = jnp.concatenate([cos_prev, cos_now], axis=0).astype(jnp.bfloat16)
        table[P_SIZE + first : P_SIZE + first + 2 * STEP, chunk] = jnp.concatenate(
            [sin_prev, sin_now], axis=0
        ).astype(jnp.bfloat16)
        if first + 2 * STEP < P_SIZE:
            cos_prev = twice * cos_now - cos_prev
            sin_prev = twice * sin_now - sin_prev
            cos_now = twice * cos_prev - cos_now
            sin_now = twice * sin_prev - sin_now


def half_of(chan, space):
    bits = chan ^ space
    for shift in (16, 8, 4, 2, 1):
        bits = bits ^ (bits >> shift)
    return bits & 1


def kernel(
    crop_hbm,
    tau_hbm,
    u_hbm,
    v_hbm,
    w_hbm,
    mine_ref,
    other_ref,
    crop_ref,
    tau_ref,
    u_ref,
    v_ref,
    w_ref,
    row_tables,
    col_tables,
    seeds,
    steps,
    beams,
    arrived,
):
    channels, count = u_ref.shape
    copies = [
        pltpu.make_async_copy(source, target, arrived.at[k])
        for k, (source, target) in enumerate(
            ((crop_hbm, crop_ref), (u_hbm, u_ref), (v_hbm, v_ref), (w_hbm, w_ref), (tau_hbm, tau_ref))
        )
    ]
    for copy in copies:
        copy.start()
    for copy in copies[:2]:
        copy.wait()
    prepare(u_ref[...], crop_ref[0], None, seeds.at[0], steps.at[0])
    for copy in copies[2:]:
        copy.wait()
    prepare(v_ref[...], crop_ref[1], w_ref[...], seeds.at[1], steps.at[1])
    beams[...] = jnp.zeros_like(beams)

    def fill(channel, slot):
        one = slice(channel, channel + 1)
        rows = slice(channel * STEP, (channel + 1) * STEP)
        for group in range(0, count // WIDTH, 2):
            chunk = slice(group * WIDTH, (group + 2) * WIDTH)
            for side, tables in enumerate((row_tables, col_tables)):
                seed = [
                    jnp.concatenate([seeds[side, k, group, rows, :], seeds[side, k, group + 1, rows, :]], axis=1)
                    for k in range(2)
                ]
                fill_table(
                    tables.at[slot],
                    chunk,
                    *seed,
                    steps[side, 0, one, chunk],
                    steps[side, 1, one, chunk],
                )

    def add(channel, slot):
        product = lax.dot_general(
            row_tables[slot], col_tables[slot], (((1,), (1,)), ((), ())), preferred_element_type=jnp.float32
        )
        beam = product[:P_SIZE, :P_SIZE] - product[P_SIZE:, P_SIZE:]
        tau = tau_ref[channel]
        power = jnp.float32(1.0)
        for term in range(TERMS):
            beams[term] += power * beam
            power = power * tau

    fill(0, 0)
    for channel in range(channels):
        if channel + 1 < channels:
            fill(channel + 1, (channel + 1) % 2)
        add(channel, channel % 2)

    squares = jnp.zeros((channels, P_SIZE), jnp.float32)
    for begin in range(0, count, P_SIZE):
        w = w_ref[:, begin : begin + P_SIZE]
        squares += w * w

    def put(low, high):
        for ref, first in ((low, 0), (high, HALF)):
            for term in range(TERMS):
                ref[term * HALF : (term + 1) * HALF, :] = beams[term, first : first + HALF, :]
            ref[TERMS * HALF :, :] = squares

    half = half_of(lax.axis_index("chan"), lax.axis_index("space"))
    pl.when(half == 0)(lambda: put(mine_ref, other_ref))
    pl.when(half == 1)(lambda: put(other_ref, mine_ref))


def finish(mine_ref, away_ref, psf_ref):
    squares = mine_ref[TERMS * HALF :, :]
    scale = 1.0 / jnp.sqrt(jnp.sum(jnp.sum(squares, axis=1, keepdims=True), axis=0, keepdims=True))

    def put(low, high):
        for ref, first in ((low, 0), (high, HALF)):
            for term in range(TERMS):
                psf_ref[term, first : first + HALF, :] = ref[term * HALF : (term + 1) * HALF, :] * scale

    half = half_of(lax.axis_index("chan"), lax.axis_index("space"))
    pl.when(half == 0)(lambda: put(mine_ref, away_ref))
    pl.when(half == 1)(lambda: put(away_ref, mine_ref))


VMEM = pl.BlockSpec(memory_space=pltpu.VMEM)
HBM = pl.BlockSpec(memory_space=pltpu.HBM)


def partial_beams(u_rows, v_cols, weights, tau, crop_start):
    channels, count = u_rows.shape
    rows = TERMS * HALF + channels
    part = jax.ShapeDtypeStruct((rows, P_SIZE), jnp.float32)
    return pl.pallas_call(
        kernel,
        out_shape=(part, part),
        in_specs=[HBM] * 5,
        out_specs=(VMEM, VMEM),
        scratch_shapes=[
            pltpu.SMEM(crop_start.shape, crop_start.dtype),
            pltpu.SMEM(tau.shape, tau.dtype),
            pltpu.VMEM(u_rows.shape, u_rows.dtype),
            pltpu.VMEM(v_cols.shape, v_cols.dtype),
            pltpu.VMEM(weights.shape, weights.dtype),
            pltpu.VMEM((2, 2 * P_SIZE, count), jnp.bfloat16),
            pltpu.VMEM((2, 2 * P_SIZE, count), jnp.bfloat16),
            pltpu.VMEM((2, 2, count // WIDTH, channels * STEP, WIDTH), jnp.float32),
            pltpu.VMEM((2, 2, channels, count), jnp.float32),
            pltpu.VMEM((TERMS, P_SIZE, P_SIZE), jnp.float32),
            pltpu.SemaphoreType.DMA((5,)),
        ],
        compiler_params=pltpu.CompilerParams(vmem_limit_bytes=16 << 20),
    )(*(pltpu.with_memory_space_constraint(x, pltpu.HBM) for x in (crop_start, tau, u_rows, v_cols, weights)))


def whole_patch(mine, away):
    return pl.pallas_call(
        finish,
        out_shape=jax.ShapeDtypeStruct((TERMS, P_SIZE, P_SIZE), jnp.float32),
        in_specs=[VMEM, VMEM],
        out_specs=VMEM,
        compiler_params=pltpu.CompilerParams(vmem_limit_bytes=4 << 20),
    )(mine, away)


def exchange_orders(chan, space):
    over_chan = [("chan", 1 << b) for b in range(1, chan.bit_length() - 1)]
    over_space = [("space", 1 << b) for b in range(space.bit_length() - 1)]
    first = []
    for k in range(max(len(over_chan), len(over_space))):
        first += over_chan[k : k + 1] + over_space[k : k + 1]
    second = list(first)
    for k in range(0, len(second) - 1, 2):
        second[k], second[k + 1] = second[k + 1], second[k]
    return first, second


def pairs_of(moves, chan, space):
    pairs = []
    for c in range(chan):
        for s in range(space):
            axis, bit = moves[half_of(c, s)]
            to = (c ^ bit ^ 1, s) if axis == "chan" else (c ^ 1, s ^ bit)
            pairs.append((c * space + s, to[0] * space + to[1]))
    return pairs


def on_device(u_rows, v_cols, weights, tau, crop_start):
    chan, space = lax.axis_size("chan"), lax.axis_size("space")
    mine, other = partial_beams(u_rows, v_cols, weights, tau, crop_start)
    partner = [(i, i ^ 1) for i in range(chan)]
    total = mine + lax.ppermute(other, "chan", partner)
    for moves in zip(*exchange_orders(chan, space)):
        total = total + lax.ppermute(total, ("chan", "space"), pairs_of(moves, chan, space))
    return whole_patch(total, lax.ppermute(total, "chan", partner))


def solution(mesh):
    in_specs = (P("chan", "space"), P("chan", "space"), P("chan", "space"), P("chan"), P())
    return jax.shard_map(on_device, mesh=mesh, in_specs=in_specs, out_specs=P(), check_vma=False)
```

time: 39.9 us -> 32.6 us (0.82)
  other arithmetic: 3.09 us -> 0.12 us
  waiting for transfers between devices: 17.8 us -> 16.4 us
  Pallas kernels: 6.61 us -> 5.76 us
  between operations: 0.73 us -> 0.02 us
  starting transfers between devices: 10.8 us -> 10.1 us
  local copies, waits for them, and re-layouts: 0.65 us -> 0 us
    concatenate x2 -> x0, other arithmetic: 1.41 us -> none  [the longest x1 0.75 us: on_device(): return jnp.concatenate([low, high], axis=1)]
    ppermute x5, waiting for transfers between devices: 16.6 us -> 15.3 us  [the longest x4 14 us: on_device(): lax.ppermute(total, ('chan', 'space'), pairs_of(moves, chan, space))]
    add x1, other arithmetic: 0.94 us -> 0.02 us  [on_device(): total = mine + lax.ppermute(other, 'chan', partner)]
    pallas_call x1 -> x2, Pallas kernels: 6.61 us -> 5.76 us  [the longest x1 4.91 us: partial_beams(): pl.pallas_call(kernel, out_shape=(part, part), in_specs=[HBM] * 5, out_sp...]
    ppermute x5, starting transfers between devices: 10.3 us -> 9.58 us  [the longest x4 9.4 us: on_device(): lax.ppermute(total, ('chan', 'space'), pairs_of(moves, chan, space))]
    unnamed x2 -> x0, local copies, waits for them, and re-layouts: 0.65 us -> none
    reduce_sum x1 -> x0, other arithmetic: 0.6 us -> none  [on_device(): beam = total[:TERMS * HALF] / jnp.sqrt(jnp.sum(total[TERMS * HALF:]))]
where the time goes in v2:
time: 32.6 us; the launch traced here: 32.4 us
  waiting for transfers between devices  16.4 us (50%)
  starting transfers between devices  10.1 us (31%)
  Pallas kernels  5.76 us (18%)
    ppermute x4, waiting for transfers between devices, on_device(): lax.ppermute(total, ('chan', 'space'), pairs_of(moves, chan, space))  14 us
    ppermute x4, starting transfers between devices, on_device(): lax.ppermute(total, ('chan', 'space'), pairs_of(moves, chan, space))  9.4 us
    pallas_call x1, Pallas kernels, partial_beams(): pl.pallas_call(kernel, out_shape=(part, part), in_specs=[HBM] * 5, out_sp...  4.91 us
    ppermute x1, waiting for transfers between devices, on_device(): return whole_patch(total, lax.ppermute(total, 'chan', partner))  1.29 us
    ppermute x1, waiting for transfers between devices, on_device(): total = mine + lax.ppermute(other, 'chan', partner)  1.03 us
    pallas_call x1, Pallas kernels, whole_patch(): pl.pallas_call(finish, out_shape=jax.ShapeDtypeStruct((TERMS, P_SIZE, P_S...  0.84 us
  transfers between devices with their start and end apart: 6, of which 6 were waited for; matrix products, arithmetic and copies ran while one was open for 0% of the time, Pallas kernels for 0%

profile of v2, /device:TPU:0, one launch (start us, length us, event | category | flops | bytes accessed | tf_op | source)
XLA Modules:
  0.0 32.4 jit_solution(17575902641021861351)
XLA Ops:
  0.0 4.9 %shard_map.55 = (f32[328,128]{1,0:T(8,128)S(1)}, f32[328,128]{1,0:T(8,128)S(1)}) custom-call(s32[2]{0:T(128)} %crop_hbm.1, f32[8]{0:T(128)} %tau_hbm.1, s32[8,2048]{1,0:T(8,128)} %u_hbm.1, s32[8,2048]{1,0:T(8,128)} %v_hbm.1, f32[8,2048]{1,0:T(8,128)} %w_hbm.1), custom_call_target="tpu_custom_call" | custom-call | tf_op jit(solution)/shard_map/pallas_call | solution.py:189
  4.9 0.6 %collective-permute-start = (f32[328,128]{1,0:T(8,128)S(1)}, f32[328,128]{1,0:T(8,128)S(1)}, u32[]{:S(2)}, u32[]{:S(2)}) collective-permute-start(f32[328,128]{1,0:T(8,128)S(1)} %get-tuple-element.8), channel_id=1, source_target_pairs={{0,4},{4,0},{8,12},{12,8},{16,20},{20,16},{24,28},{28,24},{1,5},{5... | collective-permute-start | bytes 503816 | tf_op jit(solution)/shard_map/ppermute | solution.py:247
  5.5 1.0 %collective-permute-done = f32[328,128]{1,0:T(8,128)S(1)} collective-permute-done((f32[328,128]{1,0:T(8,128)S(1)}, f32[328,128]{1,0:T(8,128)S(1)}, u32[]{:S(2)}, u32[]{:S(2)}) %collective-permute-start) | collective-permute-done | bytes 167968 | tf_op jit(solution)/shard_map/ppermute | solution.py:247
  6.5 2.6 %collective-permute-start.1 = (f32[328,128]{1,0:T(8,128)S(1)}, f32[328,128]{1,0:T(8,128)S(1)}, u32[]{:S(2)}, u32[]{:S(2)}) collective-permute-start(f32[328,128]{1,0:T(8,128)S(1)} %add.15), channel_id=1, source_target_pairs={{0,12},{1,4},{2,7},{3,15},{4,1},{5,9},{6,10},{7,2},{8,13},{9,5},{1... | collective-permute-start | bytes 503816 | tf_op jit(solution)/shard_map/ppermute | solution.py:249
  9.2 3.0 %collective-permute-done.1 = f32[328,128]{1,0:T(8,128)S(1)} collective-permute-done((f32[328,128]{1,0:T(8,128)S(1)}, f32[328,128]{1,0:T(8,128)S(1)}, u32[]{:S(2)}, u32[]{:S(2)}) %collective-permute-start.1) | collective-permute-done | bytes 167968 | tf_op jit(solution)/shard_map/ppermute | solution.py:249
  12.3 1.9 %collective-permute-start.2 = (f32[328,128]{1,0:T(8,128)S(1)}, f32[328,128]{1,0:T(8,128)S(1)}, u32[]{:S(2)}, u32[]{:S(2)}) collective-permute-start(f32[328,128]{1,0:T(8,128)S(1)} %add.16), channel_id=1, source_target_pairs={{0,5},{1,13},{2,14},{3,6},{4,8},{5,0},{6,3},{7,11},{8,4},{9,12},{1... | collective-permute-start | bytes 503816 | tf_op jit(solution)/shard_map/ppermute | solution.py:249
  14.2 3.0 %collective-permute-done.2 = f32[328,128]{1,0:T(8,128)S(1)} collective-permute-done((f32[328,128]{1,0:T(8,128)S(1)}, f32[328,128]{1,0:T(8,128)S(1)}, u32[]{:S(2)}, u32[]{:S(2)}) %collective-permute-start.2) | collective-permute-done | bytes 167968 | tf_op jit(solution)/shard_map/ppermute | solution.py:249
  17.2 1.7 %collective-permute-start.3 = (f32[328,128]{1,0:T(8,128)S(1)}, f32[328,128]{1,0:T(8,128)S(1)}, u32[]{:S(2)}, u32[]{:S(2)}) collective-permute-start(f32[328,128]{1,0:T(8,128)S(1)} %add.17), channel_id=1, source_target_pairs={{0,20},{1,7},{2,4},{3,23},{4,2},{5,17},{6,18},{7,1},{8,14},{9,29},... | collective-permute-start | bytes 503816 | tf_op jit(solution)/shard_map/ppermute | solution.py:249
  19.0 3.1 %collective-permute-done.3 = f32[328,128]{1,0:T(8,128)S(1)} collective-permute-done((f32[328,128]{1,0:T(8,128)S(1)}, f32[328,128]{1,0:T(8,128)S(1)}, u32[]{:S(2)}, u32[]{:S(2)}) %collective-permute-start.3) | collective-permute-done | bytes 167968 | tf_op jit(solution)/shard_map/ppermute | solution.py:249
  22.1 3.1 %collective-permute-start.4 = (f32[328,128]{1,0:T(8,128)S(1)}, f32[328,128]{1,0:T(8,128)S(1)}, u32[]{:S(2)}, u32[]{:S(2)}) collective-permute-start(f32[328,128]{1,0:T(8,128)S(1)} %add.18), channel_id=1, source_target_pairs={{0,6},{1,21},{2,22},{3,5},{4,16},{5,3},{6,0},{7,19},{8,28},{9,15},... | collective-permute-start | bytes 503816 | tf_op jit(solution)/shard_map/ppermute | solution.py:249
  25.2 4.8 %collective-permute-done.4 = f32[328,128]{1,0:T(8,128)S(1)} collective-permute-done((f32[328,128]{1,0:T(8,128)S(1)}, f32[328,128]{1,0:T(8,128)S(1)}, u32[]{:S(2)}, u32[]{:S(2)}) %collective-permute-start.4) | collective-permute-done | bytes 167968 | tf_op jit(solution)/shard_map/ppermute | solution.py:249
  30.1 0.2 collective-permute-start.5
  30.3 1.3 %collective-permute-done.5.away_ref = f32[328,128]{1,0:T(8,128)S(1)} collective-permute-done((f32[328,128]{1,0:T(8,128)S(1)}, f32[328,128]{1,0:T(8,128)S(1)}, u32[]{:S(2)}, u32[]{:S(2)}) %collective-permute-start.5) | collective-permute-done | bytes 167968 | tf_op jit(solution)/shard_map/ppermute | solution.py:250
  31.6 0.8 %shard_map.56 = f32[5,128,128]{2,1,0:T(8,128)} custom-call(f32[328,128]{1,0:T(8,128)S(1)} %add.19.mine_ref, f32[328,128]{1,0:T(8,128)S(1)} %collective-permute-done.5.away_ref), custom_call_target="tpu_custom_call" | custom-call | tf_op jit(solution)/shard_map/pallas_call | solution.py:212
  (5 shorter events, 0.1 us)
Async XLA Ops:
  4.9 1.6 %collective-permute-start = (f32[328,128]{1,0:T(8,128)S(1)}, f32[328,128]{1,0:T(8,128)S(1)}, u32[]{:S(2)}, u32[]{:S(2)}) collective-permute-start(f32[328,128]{1,0:T(8,128)S(1)} %get-tuple-element.8), channel_id=1, source_target_pairs={{0,4},{4,0},{8,12},{12,8},{16,20},{20,16},{24,28},{28,24},{1,5},{5... | collective-permute-start | bytes 503816 | tf_op jit(solution)/shard_map/ppermute | solution.py:247
  6.5 5.7 %collective-permute-start.1 = (f32[328,128]{1,0:T(8,128)S(1)}, f32[328,128]{1,0:T(8,128)S(1)}, u32[]{:S(2)}, u32[]{:S(2)}) collective-permute-start(f32[328,128]{1,0:T(8,128)S(1)} %add.15), channel_id=1, source_target_pairs={{0,12},{1,4},{2,7},{3,15},{4,1},{5,9},{6,10},{7,2},{8,13},{9,5},{1... | collective-permute-start | bytes 503816 | tf_op jit(solution)/shard_map/ppermute | solution.py:249
  12.3 4.9 %collective-permute-start.2 = (f32[328,128]{1,0:T(8,128)S(1)}, f32[328,128]{1,0:T(8,128)S(1)}, u32[]{:S(2)}, u32[]{:S(2)}) collective-permute-start(f32[328,128]{1,0:T(8,128)S(1)} %add.16), channel_id=1, source_target_pairs={{0,5},{1,13},{2,14},{3,6},{4,8},{5,0},{6,3},{7,11},{8,4},{9,12},{1... | collective-permute-start | bytes 503816 | tf_op jit(solution)/shard_map/ppermute | solution.py:249
  17.2 4.9 %collective-permute-start.3 = (f32[328,128]{1,0:T(8,128)S(1)}, f32[328,128]{1,0:T(8,128)S(1)}, u32[]{:S(2)}, u32[]{:S(2)}) collective-permute-start(f32[328,128]{1,0:T(8,128)S(1)} %add.17), channel_id=1, source_target_pairs={{0,20},{1,7},{2,4},{3,23},{4,2},{5,17},{6,18},{7,1},{8,14},{9,29},... | collective-permute-start | bytes 503816 | tf_op jit(solution)/shard_map/ppermute | solution.py:249
  22.1 8.0 %collective-permute-start.4 = (f32[328,128]{1,0:T(8,128)S(1)}, f32[328,128]{1,0:T(8,128)S(1)}, u32[]{:S(2)}, u32[]{:S(2)}) collective-permute-start(f32[328,128]{1,0:T(8,128)S(1)} %add.18), channel_id=1, source_target_pairs={{0,6},{1,21},{2,22},{3,5},{4,16},{5,3},{6,0},{7,19},{8,28},{9,15},... | collective-permute-start | bytes 503816 | tf_op jit(solution)/shard_map/ppermute | solution.py:249
  30.1 1.5 %collective-permute-start.5 = (f32[328,128]{1,0:T(8,128)S(1)}, f32[328,128]{1,0:T(8,128)S(1)}, u32[]{:S(2)}, u32[]{:S(2)}) collective-permute-start(f32[328,128]{1,0:T(8,128)S(1)} %add.19.mine_ref), channel_id=1, source_target_pairs={{0,4},{4,0},{8,12},{12,8},{16,20},{20,16},{24,28},{28,24},{1,5},{5... | collective-permute-start | bytes 503816 | tf_op jit(solution)/shard_map/ppermute | solution.py:250

commit v3 on v2

--- a/solution.py
+++ b/solution.py
@@ -10,7 +10,9 @@
 G = 8192
 P_SIZE = 128
 TERMS = 5
-HALF = P_SIZE // 2
+STREAMS = 2
+ROWS = P_SIZE // STREAMS
+HALF = ROWS // 2
 STEP = 8
 WIDTH = 128
 QUARTER = G // 4
@@ -82,8 +84,10 @@
     u_hbm,
     v_hbm,
     w_hbm,
-    mine_ref,
-    other_ref,
+    mine_a,
+    other_a,
+    mine_b,
+    other_b,
     crop_ref,
     tau_ref,
     u_ref,
@@ -153,29 +157,38 @@
         w = w_ref[:, begin : begin + P_SIZE]
         squares += w * w
 
-    def put(low, high):
-        for ref, first in ((low, 0), (high, HALF)):
+    mine_a[TERMS * HALF :, :] = squares
+    other_a[TERMS * HALF :, :] = squares
+
+    def put(half):
+        for k, ref in enumerate((mine_a, other_a, mine_b, other_b)):
+            first = first_row(k, half)
             for term in range(TERMS):
                 ref[term * HALF : (term + 1) * HALF, :] = beams[term, first : first + HALF, :]
-            ref[TERMS * HALF :, :] = squares
 
     half = half_of(lax.axis_index("chan"), lax.axis_index("space"))
-    pl.when(half == 0)(lambda: put(mine_ref, other_ref))
-    pl.when(half == 1)(lambda: put(other_ref, mine_ref))
-
-
-def finish(mine_ref, away_ref, psf_ref):
-    squares = mine_ref[TERMS * HALF :, :]
+    pl.when(half == 0)(lambda: put(0))
+    pl.when(half == 1)(lambda: put(1))
+
+
+def first_row(k, half):
+    return (k // 2) * ROWS + (half ^ (k % 2)) * HALF
+
+
+def finish(*refs):
+    *parts, psf_ref = refs
+    squares = parts[0][TERMS * HALF :, :]
     scale = 1.0 / jnp.sqrt(jnp.sum(jnp.sum(squares, axis=1, keepdims=True), axis=0, keepdims=True))
 
-    def put(low, high):
-        for ref, first in ((low, 0), (high, HALF)):
+    def put(half):
+        for k, ref in enumerate(parts):
+            first = first_row(k, half)
             for term in range(TERMS):
                 psf_ref[term, first : first + HALF, :] = ref[term * HALF : (term + 1) * HALF, :] * scale
 
     half = half_of(lax.axis_index("chan"), lax.axis_index("space"))
-    pl.when(half == 0)(lambda: put(mine_ref, away_ref))
-    pl.when(half == 1)(lambda: put(away_ref, mine_ref))
+    pl.when(half == 0)(lambda: put(0))
+    pl.when(half == 1)(lambda: put(1))
 
 
 VMEM = pl.BlockSpec(memory_space=pltpu.VMEM)
@@ -184,13 +197,12 @@
 
 def partial_beams(u_rows, v_cols, weights, tau, crop_start):
     channels, count = u_rows.shape
-    rows = TERMS * HALF + channels
-    part = jax.ShapeDtypeStruct((rows, P_SIZE), jnp.float32)
+    part_a, part_b = (jax.ShapeDtypeStruct((TERMS * HALF + extra, P_SIZE), jnp.float32) for extra in (channels, 0))
     return pl.pallas_call(
         kernel,
-        out_shape=(part, part),
+        out_shape=(part_a, part_a, part_b, part_b),
         in_specs=[HBM] * 5,
-        out_specs=(VMEM, VMEM),
+        out_specs=(VMEM,) * 4,
         scratch_shapes=[
             pltpu.SMEM(crop_start.shape, crop_start.dtype),
             pltpu.SMEM(tau.shape, tau.dtype),
@@ -208,26 +220,26 @@
     )(*(pltpu.with_memory_space_constraint(x, pltpu.HBM) for x in (crop_start, tau, u_rows, v_cols, weights)))
 
 
-def whole_patch(mine, away):
+def whole_patch(parts):
     return pl.pallas_call(
         finish,
         out_shape=jax.ShapeDtypeStruct((TERMS, P_SIZE, P_SIZE), jnp.float32),
-        in_specs=[VMEM, VMEM],
+        in_specs=[VMEM] * len(parts),
         out_specs=VMEM,
         compiler_params=pltpu.CompilerParams(vmem_limit_bytes=4 << 20),
-    )(mine, away)
+    )(*parts)
 
 
 def exchange_orders(chan, space):
     over_chan = [("chan", 1 << b) for b in range(1, chan.bit_length() - 1)]
     over_space = [("space", 1 << b) for b in range(space.bit_length() - 1)]
-    first = []
-    for k in range(max(len(over_chan), len(over_space))):
-        first += over_chan[k : k + 1] + over_space[k : k + 1]
-    second = list(first)
-    for k in range(0, len(second) - 1, 2):
-        second[k], second[k + 1] = second[k + 1], second[k]
-    return first, second
+    orders = []
+    for order in (over_chan + over_space, over_space + over_chan):
+        swapped = list(order)
+        for k in range(0, len(order) - 1, 2):
+            swapped[k], swapped[k + 1] = order[k + 1], order[k]
+        orders.append(list(zip(order, swapped)))
+    return orders
 
 
 def pairs_of(moves, chan, space):
@@ -242,12 +254,18 @@
 
 def on_device(u_rows, v_cols, weights, tau, crop_start):
     chan, space = lax.axis_size("chan"), lax.axis_size("space")
-    mine, other = partial_beams(u_rows, v_cols, weights, tau, crop_start)
     partner = [(i, i ^ 1) for i in range(chan)]
-    total = mine + lax.ppermute(other, "chan", partner)
-    for moves in zip(*exchange_orders(chan, space)):
-        total = total + lax.ppermute(total, ("chan", "space"), pairs_of(moves, chan, space))
-    return whole_patch(total, lax.ppermute(total, "chan", partner))
+    mine_a, other_a, mine_b, other_b = partial_beams(u_rows, v_cols, weights, tau, crop_start)
+    totals = [
+        mine + lax.ppermute(other, "chan", partner) for mine, other in ((mine_a, other_a), (mine_b, other_b))
+    ]
+    for phase in zip(*exchange_orders(chan, space)):
+        for k, moves in enumerate(phase):
+            totals[k] = totals[k] + lax.ppermute(totals[k], ("chan", "space"), pairs_of(moves, chan, space))
+    parts = []
+    for total in totals:
+        parts += [total, lax.ppermute(total, "chan", partner)]
+    return whole_patch(parts)
 
 
 def solution(mesh):

time: 32.6 us -> 29.5 us (0.905)
  waiting for transfers between devices: 16.4 us -> 5.2 us
  starting transfers between devices: 10.1 us -> 18.2 us
    ppermute x6 -> x12, waiting for transfers between devices: 16.4 us -> 5.2 us  [the longest x8 3.31 us: on_device(): lax.ppermute(totals[k], ('chan', 'space'), pairs_of(moves, chan, space))]
    ppermute x6 -> x12, starting transfers between devices: 10.1 us -> 18.2 us  [the longest x8 16.4 us: on_device(): lax.ppermute(totals[k], ('chan', 'space'), pairs_of(moves, chan, space))]
  transfers between devices with their start and end apart: 6 -> 12, of which waited for: 6 -> 6; matrix products, arithmetic and copies ran while one was open for 0% -> 0% of each run, Pallas kernels for 0% -> 0%
where the time goes in v3:
time: 29.5 us; the launch traced here: 29.3 us
  starting transfers between devices  18.2 us (62%)
  Pallas kernels  5.76 us (20%)
  waiting for transfers between devices  5.2 us (18%)
    ppermute x8, starting transfers between devices, on_device(): lax.ppermute(totals[k], ('chan', 'space'), pairs_of(moves, chan, space))  16.4 us
    pallas_call x1, Pallas kernels, partial_beams(): pl.pallas_call(kernel, out_shape=(part_a, part_a, part_b, part_b), in_spe...  4.91 us
    ppermute x8, waiting for transfers between devices, on_device(): lax.ppermute(totals[k], ('chan', 'space'), pairs_of(moves, chan, space))  3.31 us
    ppermute x2, starting transfers between devices, on_device(): parts += [total, lax.ppermute(total, 'chan', partner)]  1.14 us
    ppermute x2, waiting for transfers between devices, on_device(): parts += [total, lax.ppermute(total, 'chan', partner)]  1.04 us
    ppermute x2, waiting for transfers between devices, on_device(): lax.ppermute(other, 'chan', partner)  0.85 us
    pallas_call x1, Pallas kernels, whole_patch(): pl.pallas_call(finish, out_shape=jax.ShapeDtypeStruct((TERMS, P_SIZE, P_S...  0.84 us
    ppermute x2, starting transfers between devices, on_device(): lax.ppermute(other, 'chan', partner)  0.64 us
  transfers between devices with their start and end apart: 12, of which 6 were waited for; matrix products, arithmetic and copies ran while one was open for 0% of the time, Pallas kernels for 0%

profile of v3, /device:TPU:0, one launch (start us, length us, event | category | flops | bytes accessed | tf_op | source)
XLA Modules:
  0.0 29.3 jit_solution(3133143477764939204)
XLA Ops:
  0.0 4.9 %shard_map.55 = (f32[168,128]{1,0:T(8,128)S(1)}, f32[168,128]{1,0:T(8,128)S(1)}, f32[160,128]{1,0:T(8,128)S(1)}, f32[160,128]{1,0:T(8,128)S(1)}) custom-call(s32[2]{0:T(128)} %crop_hbm.1, f32[8]{0:T(128)} %tau_hbm.1, s32[8,2048]{1,0:T(8,128)} %u_hbm.1, s32[8,2048]{1,0:T(8,128)} %v_hbm.1, f32[8,2048]{1,0:T(8,128)} %w_hbm.1), custom_call_target="tpu_custom_call" | custom-call | tf_op jit(solution)/shard_map/pallas_call | solution.py:201
  4.9 0.6 %collective-permute-start = (f32[168,128]{1,0:T(8,128)S(1)}, f32[168,128]{1,0:T(8,128)S(1)}, u32[]{:S(2)}, u32[]{:S(2)}) collective-permute-start(f32[168,128]{1,0:T(8,128)S(1)} %get-tuple-element.10), channel_id=1, source_target_pairs={{0,4},{4,0},{8,12},{12,8},{16,20},{20,16},{24,28},{28,24},{1,5},{5... | collective-permute-start | bytes 258056 | tf_op jit(solution)/shard_map/ppermute | solution.py:260
  5.5 0.1 collective-permute-start.6
  5.6 0.8 %collective-permute-done = f32[168,128]{1,0:T(8,128)S(1)} collective-permute-done((f32[168,128]{1,0:T(8,128)S(1)}, f32[168,128]{1,0:T(8,128)S(1)}, u32[]{:S(2)}, u32[]{:S(2)}) %collective-permute-start) | collective-permute-done | bytes 86048 | tf_op jit(solution)/shard_map/ppermute | solution.py:260
  6.4 2.6 %collective-permute-start.1 = (f32[168,128]{1,0:T(8,128)S(1)}, f32[168,128]{1,0:T(8,128)S(1)}, u32[]{:S(2)}, u32[]{:S(2)}) collective-permute-start(f32[168,128]{1,0:T(8,128)S(1)} %add.30), channel_id=1, source_target_pairs={{0,12},{1,21},{2,22},{3,15},{4,16},{5,9},{6,10},{7,19},{8,28},{9,5... | collective-permute-start | bytes 258056 | tf_op jit(solution)/shard_map/ppermute | solution.py:264
  9.1 0.0 collective-permute-done.6
  9.1 1.6 %collective-permute-start.7 = (f32[160,128]{1,0:T(8,128)S(1)}, f32[160,128]{1,0:T(8,128)S(1)}, u32[]{:S(2)}, u32[]{:S(2)}) collective-permute-start(f32[160,128]{1,0:T(8,128)S(1)} %add.35), channel_id=1, source_target_pairs={{0,5},{1,7},{2,4},{3,6},{4,2},{5,0},{6,3},{7,1},{8,14},{9,12},{10,... | collective-permute-start | bytes 245768 | tf_op jit(solution)/shard_map/ppermute | solution.py:264
  10.7 0.6 %collective-permute-done.1 = f32[168,128]{1,0:T(8,128)S(1)} collective-permute-done((f32[168,128]{1,0:T(8,128)S(1)}, f32[168,128]{1,0:T(8,128)S(1)}, u32[]{:S(2)}, u32[]{:S(2)}) %collective-permute-start.1) | collective-permute-done | bytes 86048 | tf_op jit(solution)/shard_map/ppermute | solution.py:264
  11.3 2.1 %collective-permute-start.2 = (f32[168,128]{1,0:T(8,128)S(1)}, f32[168,128]{1,0:T(8,128)S(1)}, u32[]{:S(2)}, u32[]{:S(2)}) collective-permute-start(f32[168,128]{1,0:T(8,128)S(1)} %add.31), channel_id=1, source_target_pairs={{0,20},{1,13},{2,14},{3,23},{4,8},{5,17},{6,18},{7,11},{8,4},{9,29... | collective-permute-start | bytes 258056 | tf_op jit(solution)/shard_map/ppermute | solution.py:264
  13.4 0.0 collective-permute-done.7
  13.4 2.8 %collective-permute-start.8 = (f32[160,128]{1,0:T(8,128)S(1)}, f32[160,128]{1,0:T(8,128)S(1)}, u32[]{:S(2)}, u32[]{:S(2)}) collective-permute-start(f32[160,128]{1,0:T(8,128)S(1)} %add.36), channel_id=1, source_target_pairs={{0,6},{1,4},{2,7},{3,5},{4,1},{5,3},{6,0},{7,2},{8,13},{9,15},{10,... | collective-permute-start | bytes 245768 | tf_op jit(solution)/shard_map/ppermute | solution.py:264
  16.2 0.0 collective-permute-done.2
  16.2 1.2 %collective-permute-start.3 = (f32[168,128]{1,0:T(8,128)S(1)}, f32[168,128]{1,0:T(8,128)S(1)}, u32[]{:S(2)}, u32[]{:S(2)}) collective-permute-start(f32[168,128]{1,0:T(8,128)S(1)} %add.32), channel_id=1, source_target_pairs={{0,5},{1,7},{2,4},{3,6},{4,2},{5,0},{6,3},{7,1},{8,14},{9,12},{10,... | collective-permute-start | bytes 258056 | tf_op jit(solution)/shard_map/ppermute | solution.py:264
  17.4 0.9 %collective-permute-done.8 = f32[160,128]{1,0:T(8,128)S(1)} collective-permute-done((f32[160,128]{1,0:T(8,128)S(1)}, f32[160,128]{1,0:T(8,128)S(1)}, u32[]{:S(2)}, u32[]{:S(2)}) %collective-permute-start.8) | collective-permute-done | bytes 81952 | tf_op jit(solution)/shard_map/ppermute | solution.py:264
  18.4 2.0 %collective-permute-start.9 = (f32[160,128]{1,0:T(8,128)S(1)}, f32[160,128]{1,0:T(8,128)S(1)}, u32[]{:S(2)}, u32[]{:S(2)}) collective-permute-start(f32[160,128]{1,0:T(8,128)S(1)} %add.37), channel_id=1, source_target_pairs={{0,12},{1,21},{2,22},{3,15},{4,16},{5,9},{6,10},{7,19},{8,28},{9,5... | collective-permute-start | bytes 245768 | tf_op jit(solution)/shard_map/ppermute | solution.py:264
  20.4 0.0 collective-permute-done.3
  20.4 2.8 %collective-permute-start.4 = (f32[168,128]{1,0:T(8,128)S(1)}, f32[168,128]{1,0:T(8,128)S(1)}, u32[]{:S(2)}, u32[]{:S(2)}) collective-permute-start(f32[168,128]{1,0:T(8,128)S(1)} %add.33), channel_id=1, source_target_pairs={{0,6},{1,4},{2,7},{3,5},{4,1},{5,3},{6,0},{7,2},{8,13},{9,15},{10,... | collective-permute-start | bytes 258056 | tf_op jit(solution)/shard_map/ppermute | solution.py:264
  23.2 0.0 collective-permute-done.9
  23.2 1.2 %collective-permute-start.10 = (f32[160,128]{1,0:T(8,128)S(1)}, f32[160,128]{1,0:T(8,128)S(1)}, u32[]{:S(2)}, u32[]{:S(2)}) collective-permute-start(f32[160,128]{1,0:T(8,128)S(1)} %add.38), channel_id=1, source_target_pairs={{0,20},{1,13},{2,14},{3,23},{4,8},{5,17},{6,18},{7,11},{8,4},{9,29... | collective-permute-start | bytes 245768 | tf_op jit(solution)/shard_map/ppermute | solution.py:264
  24.4 1.2 %collective-permute-done.4 = f32[168,128]{1,0:T(8,128)S(1)} collective-permute-done((f32[168,128]{1,0:T(8,128)S(1)}, f32[168,128]{1,0:T(8,128)S(1)}, u32[]{:S(2)}, u32[]{:S(2)}) %collective-permute-start.4) | collective-permute-done | bytes 86048 | tf_op jit(solution)/shard_map/ppermute | solution.py:264
  25.6 0.8 %collective-permute-start.5 = (f32[168,128]{1,0:T(8,128)S(1)}, f32[168,128]{1,0:T(8,128)S(1)}, u32[]{:S(2)}, u32[]{:S(2)}) collective-permute-start(f32[168,128]{1,0:T(8,128)S(1)} %add.34.refs_0_), channel_id=1, source_target_pairs={{0,4},{4,0},{8,12},{12,8},{16,20},{20,16},{24,28},{28,24},{1,5},{5... | collective-permute-start | bytes 258056 | tf_op jit(solution)/shard_map/ppermute | solution.py:267
  26.5 0.7 %collective-permute-done.10 = f32[160,128]{1,0:T(8,128)S(1)} collective-permute-done((f32[160,128]{1,0:T(8,128)S(1)}, f32[160,128]{1,0:T(8,128)S(1)}, u32[]{:S(2)}, u32[]{:S(2)}) %collective-permute-start.10) | collective-permute-done | bytes 81952 | tf_op jit(solution)/shard_map/ppermute | solution.py:264
  27.1 0.3 %collective-permute-start.11 = (f32[160,128]{1,0:T(8,128)S(1)}, f32[160,128]{1,0:T(8,128)S(1)}, u32[]{:S(2)}, u32[]{:S(2)}) collective-permute-start(f32[160,128]{1,0:T(8,128)S(1)} %add.39.refs_2_), channel_id=1, source_target_pairs={{0,4},{4,0},{8,12},{12,8},{16,20},{20,16},{24,28},{28,24},{1,5},{5... | collective-permute-start | bytes 245768 | tf_op jit(solution)/shard_map/ppermute | solution.py:267
  27.4 1.0 %collective-permute-done.11.refs_3_ = f32[160,128]{1,0:T(8,128)S(1)} collective-permute-done((f32[160,128]{1,0:T(8,128)S(1)}, f32[160,128]{1,0:T(8,128)S(1)}, u32[]{:S(2)}, u32[]{:S(2)}) %collective-permute-start.11) | collective-permute-done | bytes 81952 | tf_op jit(solution)/shard_map/ppermute | solution.py:267
  28.5 0.0 collective-permute-done.5.refs_1_
  28.5 0.8 %shard_map.56 = f32[5,128,128]{2,1,0:T(8,128)} custom-call(f32[168,128]{1,0:T(8,128)S(1)} %add.34.refs_0_, f32[168,128]{1,0:T(8,128)S(1)} %collective-permute-done.5.refs_1_, f32[160,128]{1,0:T(8,128)S(1)} %add.39.refs_2_, f32[160,128]{1,0:T(8,128)S(1)} %collective-permute-done.11.refs_3_), custom_call_target="tpu_custom_call" | custom-call | tf_op jit(solution)/shard_map/pallas_call | solution.py:224
  (10 shorter events, 0.1 us)
Async XLA Ops:
  4.9 1.5 %collective-permute-start = (f32[168,128]{1,0:T(8,128)S(1)}, f32[168,128]{1,0:T(8,128)S(1)}, u32[]{:S(2)}, u32[]{:S(2)}) collective-permute-start(f32[168,128]{1,0:T(8,128)S(1)} %get-tuple-element.10), channel_id=1, source_target_pairs={{0,4},{4,0},{8,12},{12,8},{16,20},{20,16},{24,28},{28,24},{1,5},{5... | collective-permute-start | bytes 258056 | tf_op jit(solution)/shard_map/ppermute | solution.py:260
  5.5 3.6 %collective-permute-start.6 = (f32[160,128]{1,0:T(8,128)S(1)}, f32[160,128]{1,0:T(8,128)S(1)}, u32[]{:S(2)}, u32[]{:S(2)}) collective-permute-start(f32[160,128]{1,0:T(8,128)S(1)} %get-tuple-element.12), channel_id=1, source_target_pairs={{0,4},{4,0},{8,12},{12,8},{16,20},{20,16},{24,28},{28,24},{1,5},{5... | collective-permute-start | bytes 245768 | tf_op jit(solution)/shard_map/ppermute | solution.py:260
  6.4 4.8 %collective-permute-start.1 = (f32[168,128]{1,0:T(8,128)S(1)}, f32[168,128]{1,0:T(8,128)S(1)}, u32[]{:S(2)}, u32[]{:S(2)}) collective-permute-start(f32[168,128]{1,0:T(8,128)S(1)} %add.30), channel_id=1, source_target_pairs={{0,12},{1,21},{2,22},{3,15},{4,16},{5,9},{6,10},{7,19},{8,28},{9,5... | collective-permute-start | bytes 258056 | tf_op jit(solution)/shard_map/ppermute | solution.py:264
  9.1 4.3 %collective-permute-start.7 = (f32[160,128]{1,0:T(8,128)S(1)}, f32[160,128]{1,0:T(8,128)S(1)}, u32[]{:S(2)}, u32[]{:S(2)}) collective-permute-start(f32[160,128]{1,0:T(8,128)S(1)} %add.35), channel_id=1, source_target_pairs={{0,5},{1,7},{2,4},{3,6},{4,2},{5,0},{6,3},{7,1},{8,14},{9,12},{10,... | collective-permute-start | bytes 245768 | tf_op jit(solution)/shard_map/ppermute | solution.py:264
  11.3 5.0 %collective-permute-start.2 = (f32[168,128]{1,0:T(8,128)S(1)}, f32[168,128]{1,0:T(8,128)S(1)}, u32[]{:S(2)}, u32[]{:S(2)}) collective-permute-start(f32[168,128]{1,0:T(8,128)S(1)} %add.31), channel_id=1, source_target_pairs={{0,20},{1,13},{2,14},{3,23},{4,8},{5,17},{6,18},{7,11},{8,4},{9,29... | collective-permute-start | bytes 258056 | tf_op jit(solution)/shard_map/ppermute | solution.py:264
  13.4 4.9 %collective-permute-start.8 = (f32[160,128]{1,0:T(8,128)S(1)}, f32[160,128]{1,0:T(8,128)S(1)}, u32[]{:S(2)}, u32[]{:S(2)}) collective-permute-start(f32[160,128]{1,0:T(8,128)S(1)} %add.36), channel_id=1, source_target_pairs={{0,6},{1,4},{2,7},{3,5},{4,1},{5,3},{6,0},{7,2},{8,13},{9,15},{10,... | collective-permute-start | bytes 245768 | tf_op jit(solution)/shard_map/ppermute | solution.py:264
  16.2 4.1 %collective-permute-start.3 = (f32[168,128]{1,0:T(8,128)S(1)}, f32[168,128]{1,0:T(8,128)S(1)}, u32[]{:S(2)}, u32[]{:S(2)}) collective-permute-start(f32[168,128]{1,0:T(8,128)S(1)} %add.32), channel_id=1, source_target_pairs={{0,5},{1,7},{2,4},{3,6},{4,2},{5,0},{6,3},{7,1},{8,14},{9,12},{10,... | collective-permute-start | bytes 258056 | tf_op jit(solution)/shard_map/ppermute | solution.py:264
  18.4 4.8 %collective-permute-start.9 = (f32[160,128]{1,0:T(8,128)S(1)}, f32[160,128]{1,0:T(8,128)S(1)}, u32[]{:S(2)}, u32[]{:S(2)}) collective-permute-start(f32[160,128]{1,0:T(8,128)S(1)} %add.37), channel_id=1, source_target_pairs={{0,12},{1,21},{2,22},{3,15},{4,16},{5,9},{6,10},{7,19},{8,28},{9,5... | collective-permute-start | bytes 245768 | tf_op jit(solution)/shard_map/ppermute | solution.py:264
  20.4 5.2 %collective-permute-start.4 = (f32[168,128]{1,0:T(8,128)S(1)}, f32[168,128]{1,0:T(8,128)S(1)}, u32[]{:S(2)}, u32[]{:S(2)}) collective-permute-start(f32[168,128]{1,0:T(8,128)S(1)} %add.33), channel_id=1, source_target_pairs={{0,6},{1,4},{2,7},{3,5},{4,1},{5,3},{6,0},{7,2},{8,13},{9,15},{10,... | collective-permute-start | bytes 258056 | tf_op jit(solution)/shard_map/ppermute | solution.py:264
  23.2 3.9 %collective-permute-start.10 = (f32[160,128]{1,0:T(8,128)S(1)}, f32[160,128]{1,0:T(8,128)S(1)}, u32[]{:S(2)}, u32[]{:S(2)}) collective-permute-start(f32[160,128]{1,0:T(8,128)S(1)} %add.38), channel_id=1, source_target_pairs={{0,20},{1,13},{2,14},{3,23},{4,8},{5,17},{6,18},{7,11},{8,4},{9,29... | collective-permute-start | bytes 245768 | tf_op jit(solution)/shard_map/ppermute | solution.py:264
  25.6 2.9 %collective-permute-start.5 = (f32[168,128]{1,0:T(8,128)S(1)}, f32[168,128]{1,0:T(8,128)S(1)}, u32[]{:S(2)}, u32[]{:S(2)}) collective-permute-start(f32[168,128]{1,0:T(8,128)S(1)} %add.34.refs_0_), channel_id=1, source_target_pairs={{0,4},{4,0},{8,12},{12,8},{16,20},{20,16},{24,28},{28,24},{1,5},{5... | collective-permute-start | bytes 258056 | tf_op jit(solution)/shard_map/ppermute | solution.py:267
  27.1 1.3 %collective-permute-start.11 = (f32[160,128]{1,0:T(8,128)S(1)}, f32[160,128]{1,0:T(8,128)S(1)}, u32[]{:S(2)}, u32[]{:S(2)}) collective-permute-start(f32[160,128]{1,0:T(8,128)S(1)} %add.39.refs_2_), channel_id=1, source_target_pairs={{0,4},{4,0},{8,12},{12,8},{16,20},{20,16},{24,28},{28,24},{1,5},{5... | collective-permute-start | bytes 245768 | tf_op jit(solution)/shard_map/ppermute | solution.py:267

commit v4 on v3

--- a/solution.py
+++ b/solution.py
@@ -15,13 +15,14 @@
 HALF = ROWS // 2
 STEP = 8
 WIDTH = 128
-QUARTER = G // 4
+QUARTER = G // 2
+MIRROR = P_SIZE // 2
 
 
 def sin_cos(phase):
     quadrant = (phase + QUARTER // 2) >> (QUARTER.bit_length() - 1)
     rest = phase - quadrant * QUARTER
-    x = rest.astype(jnp.float32) * (2.0 * math.pi / G)
+    x = rest.astype(jnp.float32) * (math.pi / G)
     z = x * x
     s = x + x * z * (-1.6666654611e-1 + z * (8.3321608736e-3 + z * -1.9515295891e-4))
     c = 1.0 - 0.5 * z + z * z * (4.166664568298827e-2 + z * (-1.388731625493765e-3 + z * 2.443315711809948e-5))
@@ -33,42 +34,41 @@
     return cos_value, sin_value
 
 
-def prepare(ids, start, scale, seeds, steps):
-    cos_one, sin_one = sin_cos(ids)
-    cos_prev, sin_prev = sin_cos((ids * start) & (G - 1))
-    if scale is not None:
-        cos_prev, sin_prev = cos_prev * scale, sin_prev * scale
+def double(cos_value, sin_value):
+    square = sin_value * sin_value
+    return 1.0 - (square + square), (sin_value + sin_value) * cos_value
+
+
+def prepare(one, first, seeds, steps, group):
+    (cos_one, sin_one), (cos_prev, sin_prev) = one, first
     cos_now = cos_prev * cos_one - sin_prev * sin_one
     sin_now = sin_prev * cos_one + cos_prev * sin_one
     twice = cos_one + cos_one
-    channels, count = ids.shape
     for row in range(STEP):
-        rows = pl.ds(row, channels, stride=STEP)
-        for group in range(count // WIDTH):
-            chunk = slice(group * WIDTH, (group + 1) * WIDTH)
-            seeds[0, group, rows, :] = cos_prev[:, chunk]
-            seeds[1, group, rows, :] = sin_prev[:, chunk]
+        rows = pl.ds(row, cos_one.shape[0], stride=STEP)
+        seeds[0, group, rows, :] = cos_prev
+        seeds[1, group, rows, :] = sin_prev
         cos_prev, cos_now = cos_now, twice * cos_now - cos_prev
         sin_prev, sin_now = sin_now, twice * sin_now - sin_prev
-    steps[0], steps[1] = sin_cos((ids * STEP) & (G - 1))
-
-
-def fill_table(table, chunk, cos_prev, sin_prev, cos_step, sin_step):
-    cos_step = jnp.broadcast_to(cos_step, cos_prev.shape)
-    sin_step = jnp.broadcast_to(sin_step, cos_prev.shape)
+    chunk = slice(group * WIDTH, (group + 1) * WIDTH)
+    steps[0, :, chunk], steps[1, :, chunk] = double(*double(*double(cos_one, sin_one)))
+
+
+def fill_table(table, chunk, seed, step):
+    size = table.shape[0] // 2
+    cos_prev, sin_prev = seed
+    cos_step, sin_step = (jnp.broadcast_to(value, cos_prev.shape) for value in step)
     cos_now = cos_prev * cos_step - sin_prev * sin_step
     sin_now = sin_prev * cos_step + cos_prev * sin_step
     twice = cos_step + cos_step
-    for first in range(0, P_SIZE, 2 * STEP):
-        table[first : first + 2 * STEP, chunk] = jnp.concatenate([cos_prev, cos_now], axis=0).astype(jnp.bfloat16)
-        table[P_SIZE + first : P_SIZE + first + 2 * STEP, chunk] = jnp.concatenate(
-            [sin_prev, sin_now], axis=0
-        ).astype(jnp.bfloat16)
-        if first + 2 * STEP < P_SIZE:
+    for first in range(0, size, 2 * STEP):
+        if first:
             cos_prev = twice * cos_now - cos_prev
             sin_prev = twice * sin_now - sin_prev
             cos_now = twice * cos_prev - cos_now
             sin_now = twice * sin_prev - sin_now
+        for base, prev, now in ((first, cos_prev, cos_now), (size + first, sin_prev, sin_now)):
+            table[base : base + 2 * STEP, chunk] = jnp.concatenate([prev, now], axis=0).astype(jnp.bfloat16)
 
 
 def half_of(chan, space):
@@ -111,40 +111,41 @@
         copy.start()
     for copy in copies[:2]:
         copy.wait()
-    prepare(u_ref[...], crop_ref[0], None, seeds.at[0], steps.at[0])
+    for group in range(count // WIDTH):
+        half_step = sin_cos(u_ref[:, group * WIDTH : (group + 1) * WIDTH])
+        prepare(double(*half_step), half_step, seeds.at[0], steps.at[0], group)
     for copy in copies[2:]:
         copy.wait()
-    prepare(v_ref[...], crop_ref[1], w_ref[...], seeds.at[1], steps.at[1])
-    beams[...] = jnp.zeros_like(beams)
+    for group in range(count // WIDTH):
+        u, v, w = (ref[:, group * WIDTH : (group + 1) * WIDTH] for ref in (u_ref, v_ref, w_ref))
+        middle = u * (2 * crop_ref[0] + P_SIZE - 1) + v * (2 * crop_ref[1])
+        cos_first, sin_first = sin_cos(middle & (2 * G - 1))
+        prepare(sin_cos(v + v), (cos_first * w, sin_first * w), seeds.at[1], steps.at[1], group)
 
     def fill(channel, slot):
-        one = slice(channel, channel + 1)
-        rows = slice(channel * STEP, (channel + 1) * STEP)
+        rows = slice(STEP * channel, STEP * (channel + 1))
         for group in range(0, count // WIDTH, 2):
             chunk = slice(group * WIDTH, (group + 2) * WIDTH)
             for side, tables in enumerate((row_tables, col_tables)):
-                seed = [
-                    jnp.concatenate([seeds[side, k, group, rows, :], seeds[side, k, group + 1, rows, :]], axis=1)
-                    for k in range(2)
-                ]
-                fill_table(
-                    tables.at[slot],
-                    chunk,
-                    *seed,
-                    steps[side, 0, one, chunk],
-                    steps[side, 1, one, chunk],
-                )
+                seed, step = [], []
+                for k in range(2):
+                    pair = [seeds[side, k, group + both, rows, :] for both in range(2)]
+                    seed.append(jnp.concatenate(pair, axis=1))
+                    step.append(steps[side, k, channel : channel + 1, chunk])
+                fill_table(tables.at[slot], chunk, seed, step)
 
     def add(channel, slot):
         product = lax.dot_general(
             row_tables[slot], col_tables[slot], (((1,), (1,)), ((), ())), preferred_element_type=jnp.float32
         )
-        beam = product[:P_SIZE, :P_SIZE] - product[P_SIZE:, P_SIZE:]
+        even, odd = product[:MIRROR, :P_SIZE], product[MIRROR:, P_SIZE:]
         tau = tau_ref[channel]
-        power = jnp.float32(1.0)
+        power = None
         for term in range(TERMS):
-            beams[term] += power * beam
-            power = power * tau
+            for rows, part in ((slice(0, MIRROR), even), (slice(MIRROR, P_SIZE), odd)):
+                share = part if power is None else power * part
+                beams[term, rows] = share if channel == 0 else beams[term, rows] + share
+            power = tau if power is None else power * tau
 
     fill(0, 0)
     for channel in range(channels):
@@ -159,12 +160,22 @@
 
     mine_a[TERMS * HALF :, :] = squares
     other_a[TERMS * HALF :, :] = squares
+    back = STEP - 1 - lax.broadcasted_iota(jnp.int32, (STEP, P_SIZE), 0)
+
+    def block(term, first):
+        if first >= MIRROR:
+            d = first - MIRROR
+            return beams[term, d : d + STEP] - beams[term, MIRROR + d : MIRROR + d + STEP]
+        d = MIRROR - STEP - first
+        both = beams[term, d : d + STEP] + beams[term, MIRROR + d : MIRROR + d + STEP]
+        return jnp.take_along_axis(both, back, axis=0)
 
     def put(half):
         for k, ref in enumerate((mine_a, other_a, mine_b, other_b)):
             first = first_row(k, half)
             for term in range(TERMS):
-                ref[term * HALF : (term + 1) * HALF, :] = beams[term, first : first + HALF, :]
+                for row in range(0, HALF, STEP):
+                    ref[term * HALF + row : term * HALF + row + STEP, :] = block(term, first + row)
 
     half = half_of(lax.axis_index("chan"), lax.axis_index("space"))
     pl.when(half == 0)(lambda: put(0))
@@ -209,9 +220,9 @@
             pltpu.VMEM(u_rows.shape, u_rows.dtype),
             pltpu.VMEM(v_cols.shape, v_cols.dtype),
             pltpu.VMEM(weights.shape, weights.dtype),
+            pltpu.VMEM((2, 2 * MIRROR, count), jnp.bfloat16),
             pltpu.VMEM((2, 2 * P_SIZE, count), jnp.bfloat16),
-            pltpu.VMEM((2, 2 * P_SIZE, count), jnp.bfloat16),
-            pltpu.VMEM((2, 2, count // WIDTH, channels * STEP, WIDTH), jnp.float32),
+            pltpu.VMEM((2, 2, count // WIDTH, STEP * channels, WIDTH), jnp.float32),
             pltpu.VMEM((2, 2, channels, count), jnp.float32),
             pltpu.VMEM((TERMS, P_SIZE, P_SIZE), jnp.float32),
             pltpu.SemaphoreType.DMA((5,)),

time: 29.5 us -> 28.7 us (0.973)
  Pallas kernels: 5.76 us -> 4.98 us
    pallas_call x1, Pallas kernels: 4.91 us -> 4.13 us  [partial_beams(): pl.pallas_call(kernel, out_shape=(part_a, part_a, part_b, part_b), in_spe...]
where the time goes in v4:
time: 28.7 us; the launch traced here: 28.5 us
  starting transfers between devices  18.2 us (63%)
  waiting for transfers between devices  5.22 us (18%)
  Pallas kernels  4.98 us (17%)
    ppermute x8, starting transfers between devices, on_device(): lax.ppermute(totals[k], ('chan', 'space'), pairs_of(moves, chan, space))  16.4 us
    pallas_call x1, Pallas kernels, partial_beams(): pl.pallas_call(kernel, out_shape=(part_a, part_a, part_b, part_b), in_spe...  4.13 us
    ppermute x8, waiting for transfers between devices, on_device(): lax.ppermute(totals[k], ('chan', 'space'), pairs_of(moves, chan, space))  3.31 us
    ppermute x2, starting transfers between devices, on_device(): parts += [total, lax.ppermute(total, 'chan', partner)]  1.13 us
    ppermute x2, waiting for transfers between devices, on_device(): parts += [total, lax.ppermute(total, 'chan', partner)]  1.06 us
    ppermute x2, waiting for transfers between devices, on_device(): lax.ppermute(other, 'chan', partner)  0.85 us
    pallas_call x1, Pallas kernels, whole_patch(): pl.pallas_call(finish, out_shape=jax.ShapeDtypeStruct((TERMS, P_SIZE, P_S...  0.84 us
    ppermute x2, starting transfers between devices, on_device(): lax.ppermute(other, 'chan', partner)  0.63 us
  transfers between devices with their start and end apart: 12, of which 6 were waited for; matrix products, arithmetic and copies ran while one was open for 0% of the time, Pallas kernels for 0%

profile of v4, /device:TPU:0, one launch (start us, length us, event | category | flops | bytes accessed | tf_op | source)
XLA Modules:
  0.0 28.5 jit_solution(15632886562280626937)
XLA Ops:
  0.0 4.1 %shard_map.55 = (f32[168,128]{1,0:T(8,128)S(1)}, f32[168,128]{1,0:T(8,128)S(1)}, f32[160,128]{1,0:T(8,128)S(1)}, f32[160,128]{1,0:T(8,128)S(1)}) custom-call(s32[2]{0:T(128)} %crop_hbm.1, f32[8]{0:T(128)} %tau_hbm.1, s32[8,2048]{1,0:T(8,128)} %u_hbm.1, s32[8,2048]{1,0:T(8,128)} %v_hbm.1, f32[8,2048]{1,0:T(8,128)} %w_hbm.1), custom_call_target="tpu_custom_call" | custom-call | tf_op jit(solution)/shard_map/pallas_call | solution.py:212
  4.1 0.6 %collective-permute-start = (f32[168,128]{1,0:T(8,128)S(1)}, f32[168,128]{1,0:T(8,128)S(1)}, u32[]{:S(2)}, u32[]{:S(2)}) collective-permute-start(f32[168,128]{1,0:T(8,128)S(1)} %get-tuple-element.10), channel_id=1, source_target_pairs={{0,4},{4,0},{8,12},{12,8},{16,20},{20,16},{24,28},{28,24},{1,5},{5... | collective-permute-start | bytes 258056 | tf_op jit(solution)/shard_map/ppermute | solution.py:271
  4.7 0.1 collective-permute-start.6
  4.8 0.8 %collective-permute-done = f32[168,128]{1,0:T(8,128)S(1)} collective-permute-done((f32[168,128]{1,0:T(8,128)S(1)}, f32[168,128]{1,0:T(8,128)S(1)}, u32[]{:S(2)}, u32[]{:S(2)}) %collective-permute-start) | collective-permute-done | bytes 86048 | tf_op jit(solution)/shard_map/ppermute | solution.py:271
  5.6 2.7 %collective-permute-start.1 = (f32[168,128]{1,0:T(8,128)S(1)}, f32[168,128]{1,0:T(8,128)S(1)}, u32[]{:S(2)}, u32[]{:S(2)}) collective-permute-start(f32[168,128]{1,0:T(8,128)S(1)} %add.30), channel_id=1, source_target_pairs={{0,12},{1,21},{2,22},{3,15},{4,16},{5,9},{6,10},{7,19},{8,28},{9,5... | collective-permute-start | bytes 258056 | tf_op jit(solution)/shard_map/ppermute | solution.py:275
  8.3 0.0 collective-permute-done.6
  8.3 1.6 %collective-permute-start.7 = (f32[160,128]{1,0:T(8,128)S(1)}, f32[160,128]{1,0:T(8,128)S(1)}, u32[]{:S(2)}, u32[]{:S(2)}) collective-permute-start(f32[160,128]{1,0:T(8,128)S(1)} %add.35), channel_id=1, source_target_pairs={{0,5},{1,7},{2,4},{3,6},{4,2},{5,0},{6,3},{7,1},{8,14},{9,12},{10,... | collective-permute-start | bytes 245768 | tf_op jit(solution)/shard_map/ppermute | solution.py:275
  9.9 0.6 %collective-permute-done.1 = f32[168,128]{1,0:T(8,128)S(1)} collective-permute-done((f32[168,128]{1,0:T(8,128)S(1)}, f32[168,128]{1,0:T(8,128)S(1)}, u32[]{:S(2)}, u32[]{:S(2)}) %collective-permute-start.1) | collective-permute-done | bytes 86048 | tf_op jit(solution)/shard_map/ppermute | solution.py:275
  10.5 2.1 %collective-permute-start.2 = (f32[168,128]{1,0:T(8,128)S(1)}, f32[168,128]{1,0:T(8,128)S(1)}, u32[]{:S(2)}, u32[]{:S(2)}) collective-permute-start(f32[168,128]{1,0:T(8,128)S(1)} %add.31), channel_id=1, source_target_pairs={{0,20},{1,13},{2,14},{3,23},{4,8},{5,17},{6,18},{7,11},{8,4},{9,29... | collective-permute-start | bytes 258056 | tf_op jit(solution)/shard_map/ppermute | solution.py:275
  12.6 0.0 collective-permute-done.7
  12.6 2.8 %collective-permute-start.8 = (f32[160,128]{1,0:T(8,128)S(1)}, f32[160,128]{1,0:T(8,128)S(1)}, u32[]{:S(2)}, u32[]{:S(2)}) collective-permute-start(f32[160,128]{1,0:T(8,128)S(1)} %add.36), channel_id=1, source_target_pairs={{0,6},{1,4},{2,7},{3,5},{4,1},{5,3},{6,0},{7,2},{8,13},{9,15},{10,... | collective-permute-start | bytes 245768 | tf_op jit(solution)/shard_map/ppermute | solution.py:275
  15.4 0.0 collective-permute-done.2
  15.4 1.2 %collective-permute-start.3 = (f32[168,128]{1,0:T(8,128)S(1)}, f32[168,128]{1,0:T(8,128)S(1)}, u32[]{:S(2)}, u32[]{:S(2)}) collective-permute-start(f32[168,128]{1,0:T(8,128)S(1)} %add.32), channel_id=1, source_target_pairs={{0,5},{1,7},{2,4},{3,6},{4,2},{5,0},{6,3},{7,1},{8,14},{9,12},{10,... | collective-permute-start | bytes 258056 | tf_op jit(solution)/shard_map/ppermute | solution.py:275
  16.7 0.9 %collective-permute-done.8 = f32[160,128]{1,0:T(8,128)S(1)} collective-permute-done((f32[160,128]{1,0:T(8,128)S(1)}, f32[160,128]{1,0:T(8,128)S(1)}, u32[]{:S(2)}, u32[]{:S(2)}) %collective-permute-start.8) | collective-permute-done | bytes 81952 | tf_op jit(solution)/shard_map/ppermute | solution.py:275
  17.6 2.0 %collective-permute-start.9 = (f32[160,128]{1,0:T(8,128)S(1)}, f32[160,128]{1,0:T(8,128)S(1)}, u32[]{:S(2)}, u32[]{:S(2)}) collective-permute-start(f32[160,128]{1,0:T(8,128)S(1)} %add.37), channel_id=1, source_target_pairs={{0,12},{1,21},{2,22},{3,15},{4,16},{5,9},{6,10},{7,19},{8,28},{9,5... | collective-permute-start | bytes 245768 | tf_op jit(solution)/shard_map/ppermute | solution.py:275
  19.6 0.0 collective-permute-done.3
  19.6 2.8 %collective-permute-start.4 = (f32[168,128]{1,0:T(8,128)S(1)}, f32[168,128]{1,0:T(8,128)S(1)}, u32[]{:S(2)}, u32[]{:S(2)}) collective-permute-start(f32[168,128]{1,0:T(8,128)S(1)} %add.33), channel_id=1, source_target_pairs={{0,6},{1,4},{2,7},{3,5},{4,1},{5,3},{6,0},{7,2},{8,13},{9,15},{10,... | collective-permute-start | bytes 258056 | tf_op jit(solution)/shard_map/ppermute | solution.py:275
  22.4 0.0 collective-permute-done.9
  22.4 1.2 %collective-permute-start.10 = (f32[160,128]{1,0:T(8,128)S(1)}, f32[160,128]{1,0:T(8,128)S(1)}, u32[]{:S(2)}, u32[]{:S(2)}) collective-permute-start(f32[160,128]{1,0:T(8,128)S(1)} %add.38), channel_id=1, source_target_pairs={{0,20},{1,13},{2,14},{3,23},{4,8},{5,17},{6,18},{7,11},{8,4},{9,29... | collective-permute-start | bytes 245768 | tf_op jit(solution)/shard_map/ppermute | solution.py:275
  23.6 1.2 %collective-permute-done.4 = f32[168,128]{1,0:T(8,128)S(1)} collective-permute-done((f32[168,128]{1,0:T(8,128)S(1)}, f32[168,128]{1,0:T(8,128)S(1)}, u32[]{:S(2)}, u32[]{:S(2)}) %collective-permute-start.4) | collective-permute-done | bytes 86048 | tf_op jit(solution)/shard_map/ppermute | solution.py:275
  24.8 0.8 %collective-permute-start.5 = (f32[168,128]{1,0:T(8,128)S(1)}, f32[168,128]{1,0:T(8,128)S(1)}, u32[]{:S(2)}, u32[]{:S(2)}) collective-permute-start(f32[168,128]{1,0:T(8,128)S(1)} %add.34.refs_0_), channel_id=1, source_target_pairs={{0,4},{4,0},{8,12},{12,8},{16,20},{20,16},{24,28},{28,24},{1,5},{5... | collective-permute-start | bytes 258056 | tf_op jit(solution)/shard_map/ppermute | solution.py:278
  25.7 0.7 %collective-permute-done.10 = f32[160,128]{1,0:T(8,128)S(1)} collective-permute-done((f32[160,128]{1,0:T(8,128)S(1)}, f32[160,128]{1,0:T(8,128)S(1)}, u32[]{:S(2)}, u32[]{:S(2)}) %collective-permute-start.10) | collective-permute-done | bytes 81952 | tf_op jit(solution)/shard_map/ppermute | solution.py:275
  26.3 0.3 %collective-permute-start.11 = (f32[160,128]{1,0:T(8,128)S(1)}, f32[160,128]{1,0:T(8,128)S(1)}, u32[]{:S(2)}, u32[]{:S(2)}) collective-permute-start(f32[160,128]{1,0:T(8,128)S(1)} %add.39.refs_2_), channel_id=1, source_target_pairs={{0,4},{4,0},{8,12},{12,8},{16,20},{20,16},{24,28},{28,24},{1,5},{5... | collective-permute-start | bytes 245768 | tf_op jit(solution)/shard_map/ppermute | solution.py:278
  26.6 1.1 %collective-permute-done.11.refs_3_ = f32[160,128]{1,0:T(8,128)S(1)} collective-permute-done((f32[160,128]{1,0:T(8,128)S(1)}, f32[160,128]{1,0:T(8,128)S(1)}, u32[]{:S(2)}, u32[]{:S(2)}) %collective-permute-start.11) | collective-permute-done | bytes 81952 | tf_op jit(solution)/shard_map/ppermute | solution.py:278
  27.7 0.0 collective-permute-done.5.refs_1_
  27.7 0.8 %shard_map.56 = f32[5,128,128]{2,1,0:T(8,128)} custom-call(f32[168,128]{1,0:T(8,128)S(1)} %add.34.refs_0_, f32[168,128]{1,0:T(8,128)S(1)} %collective-permute-done.5.refs_1_, f32[160,128]{1,0:T(8,128)S(1)} %add.39.refs_2_, f32[160,128]{1,0:T(8,128)S(1)} %collective-permute-done.11.refs_3_), custom_call_target="tpu_custom_call" | custom-call | tf_op jit(solution)/shard_map/pallas_call | solution.py:235
  (10 shorter events, 0.1 us)
Async XLA Ops:
  4.1 1.5 %collective-permute-start = (f32[168,128]{1,0:T(8,128)S(1)}, f32[168,128]{1,0:T(8,128)S(1)}, u32[]{:S(2)}, u32[]{:S(2)}) collective-permute-start(f32[168,128]{1,0:T(8,128)S(1)} %get-tuple-element.10), channel_id=1, source_target_pairs={{0,4},{4,0},{8,12},{12,8},{16,20},{20,16},{24,28},{28,24},{1,5},{5... | collective-permute-start | bytes 258056 | tf_op jit(solution)/shard_map/ppermute | solution.py:271
  4.7 3.6 %collective-permute-start.6 = (f32[160,128]{1,0:T(8,128)S(1)}, f32[160,128]{1,0:T(8,128)S(1)}, u32[]{:S(2)}, u32[]{:S(2)}) collective-permute-start(f32[160,128]{1,0:T(8,128)S(1)} %get-tuple-element.12), channel_id=1, source_target_pairs={{0,4},{4,0},{8,12},{12,8},{16,20},{20,16},{24,28},{28,24},{1,5},{5... | collective-permute-start | bytes 245768 | tf_op jit(solution)/shard_map/ppermute | solution.py:271
  5.6 4.8 %collective-permute-start.1 = (f32[168,128]{1,0:T(8,128)S(1)}, f32[168,128]{1,0:T(8,128)S(1)}, u32[]{:S(2)}, u32[]{:S(2)}) collective-permute-start(f32[168,128]{1,0:T(8,128)S(1)} %add.30), channel_id=1, source_target_pairs={{0,12},{1,21},{2,22},{3,15},{4,16},{5,9},{6,10},{7,19},{8,28},{9,5... | collective-permute-start | bytes 258056 | tf_op jit(solution)/shard_map/ppermute | solution.py:275
  8.3 4.3 %collective-permute-start.7 = (f32[160,128]{1,0:T(8,128)S(1)}, f32[160,128]{1,0:T(8,128)S(1)}, u32[]{:S(2)}, u32[]{:S(2)}) collective-permute-start(f32[160,128]{1,0:T(8,128)S(1)} %add.35), channel_id=1, source_target_pairs={{0,5},{1,7},{2,4},{3,6},{4,2},{5,0},{6,3},{7,1},{8,14},{9,12},{10,... | collective-permute-start | bytes 245768 | tf_op jit(solution)/shard_map/ppermute | solution.py:275
  10.5 4.9 %collective-permute-start.2 = (f32[168,128]{1,0:T(8,128)S(1)}, f32[168,128]{1,0:T(8,128)S(1)}, u32[]{:S(2)}, u32[]{:S(2)}) collective-permute-start(f32[168,128]{1,0:T(8,128)S(1)} %add.31), channel_id=1, source_target_pairs={{0,20},{1,13},{2,14},{3,23},{4,8},{5,17},{6,18},{7,11},{8,4},{9,29... | collective-permute-start | bytes 258056 | tf_op jit(solution)/shard_map/ppermute | solution.py:275
  12.6 4.9 %collective-permute-start.8 = (f32[160,128]{1,0:T(8,128)S(1)}, f32[160,128]{1,0:T(8,128)S(1)}, u32[]{:S(2)}, u32[]{:S(2)}) collective-permute-start(f32[160,128]{1,0:T(8,128)S(1)} %add.36), channel_id=1, source_target_pairs={{0,6},{1,4},{2,7},{3,5},{4,1},{5,3},{6,0},{7,2},{8,13},{9,15},{10,... | collective-permute-start | bytes 245768 | tf_op jit(solution)/shard_map/ppermute | solution.py:275
  15.4 4.1 %collective-permute-start.3 = (f32[168,128]{1,0:T(8,128)S(1)}, f32[168,128]{1,0:T(8,128)S(1)}, u32[]{:S(2)}, u32[]{:S(2)}) collective-permute-start(f32[168,128]{1,0:T(8,128)S(1)} %add.32), channel_id=1, source_target_pairs={{0,5},{1,7},{2,4},{3,6},{4,2},{5,0},{6,3},{7,1},{8,14},{9,12},{10,... | collective-permute-start | bytes 258056 | tf_op jit(solution)/shard_map/ppermute | solution.py:275
  17.6 4.8 %collective-permute-start.9 = (f32[160,128]{1,0:T(8,128)S(1)}, f32[160,128]{1,0:T(8,128)S(1)}, u32[]{:S(2)}, u32[]{:S(2)}) collective-permute-start(f32[160,128]{1,0:T(8,128)S(1)} %add.37), channel_id=1, source_target_pairs={{0,12},{1,21},{2,22},{3,15},{4,16},{5,9},{6,10},{7,19},{8,28},{9,5... | collective-permute-start | bytes 245768 | tf_op jit(solution)/shard_map/ppermute | solution.py:275
  19.6 5.2 %collective-permute-start.4 = (f32[168,128]{1,0:T(8,128)S(1)}, f32[168,128]{1,0:T(8,128)S(1)}, u32[]{:S(2)}, u32[]{:S(2)}) collective-permute-start(f32[168,128]{1,0:T(8,128)S(1)} %add.33), channel_id=1, source_target_pairs={{0,6},{1,4},{2,7},{3,5},{4,1},{5,3},{6,0},{7,2},{8,13},{9,15},{10,... | collective-permute-start | bytes 258056 | tf_op jit(solution)/shard_map/ppermute | solution.py:275
  22.4 3.9 %collective-permute-start.10 = (f32[160,128]{1,0:T(8,128)S(1)}, f32[160,128]{1,0:T(8,128)S(1)}, u32[]{:S(2)}, u32[]{:S(2)}) collective-permute-start(f32[160,128]{1,0:T(8,128)S(1)} %add.38), channel_id=1, source_target_pairs={{0,20},{1,13},{2,14},{3,23},{4,8},{5,17},{6,18},{7,11},{8,4},{9,29... | collective-permute-start | bytes 245768 | tf_op jit(solution)/shard_map/ppermute | solution.py:275
  24.8 2.9 %collective-permute-start.5 = (f32[168,128]{1,0:T(8,128)S(1)}, f32[168,128]{1,0:T(8,128)S(1)}, u32[]{:S(2)}, u32[]{:S(2)}) collective-permute-start(f32[168,128]{1,0:T(8,128)S(1)} %add.34.refs_0_), channel_id=1, source_target_pairs={{0,4},{4,0},{8,12},{12,8},{16,20},{20,16},{24,28},{28,24},{1,5},{5... | collective-permute-start | bytes 258056 | tf_op jit(solution)/shard_map/ppermute | solution.py:278
  26.3 1.3 %collective-permute-start.11 = (f32[160,128]{1,0:T(8,128)S(1)}, f32[160,128]{1,0:T(8,128)S(1)}, u32[]{:S(2)}, u32[]{:S(2)}) collective-permute-start(f32[160,128]{1,0:T(8,128)S(1)} %add.39.refs_2_), channel_id=1, source_target_pairs={{0,4},{4,0},{8,12},{12,8},{16,20},{20,16},{24,28},{28,24},{1,5},{5... | collective-permute-start | bytes 245768 | tf_op jit(solution)/shard_map/ppermute | solution.py:278

commit v5 on v4

--- a/solution.py
+++ b/solution.py
@@ -16,7 +16,6 @@
 STEP = 8
 WIDTH = 128
 QUARTER = G // 2
-MIRROR = P_SIZE // 2
 
 
 def sin_cos(phase):
@@ -112,14 +111,13 @@
     for copy in copies[:2]:
         copy.wait()
     for group in range(count // WIDTH):
-        half_step = sin_cos(u_ref[:, group * WIDTH : (group + 1) * WIDTH])
-        prepare(double(*half_step), half_step, seeds.at[0], steps.at[0], group)
+        u = u_ref[:, group * WIDTH : (group + 1) * WIDTH]
+        prepare(sin_cos(u + u), sin_cos((u * (2 * crop_ref[0])) & (2 * G - 1)), seeds.at[0], steps.at[0], group)
     for copy in copies[2:]:
         copy.wait()
     for group in range(count // WIDTH):
-        u, v, w = (ref[:, group * WIDTH : (group + 1) * WIDTH] for ref in (u_ref, v_ref, w_ref))
-        middle = u * (2 * crop_ref[0] + P_SIZE - 1) + v * (2 * crop_ref[1])
-        cos_first, sin_first = sin_cos(middle & (2 * G - 1))
+        v, w = (ref[:, group * WIDTH : (group + 1) * WIDTH] for ref in (v_ref, w_ref))
+        cos_first, sin_first = sin_cos((v * (2 * crop_ref[1])) & (2 * G - 1))
         prepare(sin_cos(v + v), (cos_first * w, sin_first * w), seeds.at[1], steps.at[1], group)
 
     def fill(channel, slot):
@@ -138,13 +136,12 @@
         product = lax.dot_general(
             row_tables[slot], col_tables[slot], (((1,), (1,)), ((), ())), preferred_element_type=jnp.float32
         )
-        even, odd = product[:MIRROR, :P_SIZE], product[MIRROR:, P_SIZE:]
+        beam = product[:P_SIZE, :P_SIZE] - product[P_SIZE:, P_SIZE:]
         tau = tau_ref[channel]
         power = None
         for term in range(TERMS):
-            for rows, part in ((slice(0, MIRROR), even), (slice(MIRROR, P_SIZE), odd)):
-                share = part if power is None else power * part
-                beams[term, rows] = share if channel == 0 else beams[term, rows] + share
+            share = beam if power is None else power * beam
+            beams[term] = share if channel == 0 else beams[term] + share
             power = tau if power is None else power * tau
 
     fill(0, 0)
@@ -160,22 +157,12 @@
 
     mine_a[TERMS * HALF :, :] = squares
     other_a[TERMS * HALF :, :] = squares
-    back = STEP - 1 - lax.broadcasted_iota(jnp.int32, (STEP, P_SIZE), 0)
-
-    def block(term, first):
-        if first >= MIRROR:
-            d = first - MIRROR
-            return beams[term, d : d + STEP] - beams[term, MIRROR + d : MIRROR + d + STEP]
-        d = MIRROR - STEP - first
-        both = beams[term, d : d + STEP] + beams[term, MIRROR + d : MIRROR + d + STEP]
-        return jnp.take_along_axis(both, back, axis=0)
 
     def put(half):
         for k, ref in enumerate((mine_a, other_a, mine_b, other_b)):
             first = first_row(k, half)
             for term in range(TERMS):
-                for row in range(0, HALF, STEP):
-                    ref[term * HALF + row : term * HALF + row + STEP, :] = block(term, first + row)
+                ref[term * HALF : (term + 1) * HALF, :] = beams[term, first : first + HALF, :]
 
     half = half_of(lax.axis_index("chan"), lax.axis_index("space"))
     pl.when(half == 0)(lambda: put(0))
@@ -220,7 +207,7 @@
             pltpu.VMEM(u_rows.shape, u_rows.dtype),
             pltpu.VMEM(v_cols.shape, v_cols.dtype),
             pltpu.VMEM(weights.shape, weights.dtype),
-            pltpu.VMEM((2, 2 * MIRROR, count), jnp.bfloat16),
+            pltpu.VMEM((2, 2 * P_SIZE, count), jnp.bfloat16),
             pltpu.VMEM((2, 2 * P_SIZE, count), jnp.bfloat16),
             pltpu.VMEM((2, 2, count // WIDTH, STEP * channels, WIDTH), jnp.float32),
             pltpu.VMEM((2, 2, channels, count), jnp.float32),

time: 28.7 us -> 29.2 us (1.017)
  Pallas kernels: 4.98 us -> 5.49 us
    pallas_call x1, Pallas kernels: 4.13 us -> 4.64 us  [partial_beams(): pl.pallas_call(kernel, out_shape=(part_a, part_a, part_b, part_b), in_spe...]
where the time goes in v5:
time: 29.2 us; the launch traced here: 29.1 us
  starting transfers between devices  18.2 us (62%)
  Pallas kernels  5.49 us (19%)
  waiting for transfers between devices  5.22 us (18%)
    ppermute x8, starting transfers between devices, on_device(): lax.ppermute(totals[k], ('chan', 'space'), pairs_of(moves, chan, space))  16.4 us
    pallas_call x1, Pallas kernels, partial_beams(): pl.pallas_call(kernel, out_shape=(part_a, part_a, part_b, part_b), in_spe...  4.64 us
    ppermute x8, waiting for transfers between devices, on_device(): lax.ppermute(totals[k], ('chan', 'space'), pairs_of(moves, chan, space))  3.32 us
    ppermute x2, starting transfers between devices, on_device(): parts += [total, lax.ppermute(total, 'chan', partner)]  1.13 us
    ppermute x2, waiting for transfers between devices, on_device(): parts += [total, lax.ppermute(total, 'chan', partner)]  1.05 us
    ppermute x2, waiting for transfers between devices, on_device(): lax.ppermute(other, 'chan', partner)  0.85 us
    pallas_call x1, Pallas kernels, whole_patch(): pl.pallas_call(finish, out_shape=jax.ShapeDtypeStruct((TERMS, P_SIZE, P_S...  0.84 us
    ppermute x2, starting transfers between devices, on_device(): lax.ppermute(other, 'chan', partner)  0.64 us
  transfers between devices with their start and end apart: 12, of which 6 were waited for; matrix products, arithmetic and copies ran while one was open for 0% of the time, Pallas kernels for 0%

profile of v5, /device:TPU:0, one launch (start us, length us, event | category | flops | bytes accessed | tf_op | source)
XLA Modules:
  0.0 29.1 jit_solution(16513916010176602266)
XLA Ops:
  0.0 4.6 %shard_map.55 = (f32[168,128]{1,0:T(8,128)S(1)}, f32[168,128]{1,0:T(8,128)S(1)}, f32[160,128]{1,0:T(8,128)S(1)}, f32[160,128]{1,0:T(8,128)S(1)}) custom-call(s32[2]{0:T(128)} %crop_hbm.1, f32[8]{0:T(128)} %tau_hbm.1, s32[8,2048]{1,0:T(8,128)} %u_hbm.1, s32[8,2048]{1,0:T(8,128)} %v_hbm.1, f32[8,2048]{1,0:T(8,128)} %w_hbm.1), custom_call_target="tpu_custom_call" | custom-call | tf_op jit(solution)/shard_map/pallas_call | solution.py:199
  4.7 0.6 %collective-permute-start = (f32[168,128]{1,0:T(8,128)S(1)}, f32[168,128]{1,0:T(8,128)S(1)}, u32[]{:S(2)}, u32[]{:S(2)}) collective-permute-start(f32[168,128]{1,0:T(8,128)S(1)} %get-tuple-element.10), channel_id=1, source_target_pairs={{0,4},{4,0},{8,12},{12,8},{16,20},{20,16},{24,28},{28,24},{1,5},{5... | collective-permute-start | bytes 258056 | tf_op jit(solution)/shard_map/ppermute | solution.py:258
  5.2 0.1 collective-permute-start.6
  5.3 0.8 %collective-permute-done = f32[168,128]{1,0:T(8,128)S(1)} collective-permute-done((f32[168,128]{1,0:T(8,128)S(1)}, f32[168,128]{1,0:T(8,128)S(1)}, u32[]{:S(2)}, u32[]{:S(2)}) %collective-permute-start) | collective-permute-done | bytes 86048 | tf_op jit(solution)/shard_map/ppermute | solution.py:258
  6.2 2.7 %collective-permute-start.1 = (f32[168,128]{1,0:T(8,128)S(1)}, f32[168,128]{1,0:T(8,128)S(1)}, u32[]{:S(2)}, u32[]{:S(2)}) collective-permute-start(f32[168,128]{1,0:T(8,128)S(1)} %add.30), channel_id=1, source_target_pairs={{0,12},{1,21},{2,22},{3,15},{4,16},{5,9},{6,10},{7,19},{8,28},{9,5... | collective-permute-start | bytes 258056 | tf_op jit(solution)/shard_map/ppermute | solution.py:262
  8.8 0.0 collective-permute-done.6
  8.8 1.6 %collective-permute-start.7 = (f32[160,128]{1,0:T(8,128)S(1)}, f32[160,128]{1,0:T(8,128)S(1)}, u32[]{:S(2)}, u32[]{:S(2)}) collective-permute-start(f32[160,128]{1,0:T(8,128)S(1)} %add.35), channel_id=1, source_target_pairs={{0,5},{1,7},{2,4},{3,6},{4,2},{5,0},{6,3},{7,1},{8,14},{9,12},{10,... | collective-permute-start | bytes 245768 | tf_op jit(solution)/shard_map/ppermute | solution.py:262
  10.4 0.6 %collective-permute-done.1 = f32[168,128]{1,0:T(8,128)S(1)} collective-permute-done((f32[168,128]{1,0:T(8,128)S(1)}, f32[168,128]{1,0:T(8,128)S(1)}, u32[]{:S(2)}, u32[]{:S(2)}) %collective-permute-start.1) | collective-permute-done | bytes 86048 | tf_op jit(solution)/shard_map/ppermute | solution.py:262
  11.0 2.1 %collective-permute-start.2 = (f32[168,128]{1,0:T(8,128)S(1)}, f32[168,128]{1,0:T(8,128)S(1)}, u32[]{:S(2)}, u32[]{:S(2)}) collective-permute-start(f32[168,128]{1,0:T(8,128)S(1)} %add.31), channel_id=1, source_target_pairs={{0,20},{1,13},{2,14},{3,23},{4,8},{5,17},{6,18},{7,11},{8,4},{9,29... | collective-permute-start | bytes 258056 | tf_op jit(solution)/shard_map/ppermute | solution.py:262
  13.1 0.0 collective-permute-done.7
  13.1 2.8 %collective-permute-start.8 = (f32[160,128]{1,0:T(8,128)S(1)}, f32[160,128]{1,0:T(8,128)S(1)}, u32[]{:S(2)}, u32[]{:S(2)}) collective-permute-start(f32[160,128]{1,0:T(8,128)S(1)} %add.36), channel_id=1, source_target_pairs={{0,6},{1,4},{2,7},{3,5},{4,1},{5,3},{6,0},{7,2},{8,13},{9,15},{10,... | collective-permute-start | bytes 245768 | tf_op jit(solution)/shard_map/ppermute | solution.py:262
  15.9 0.0 collective-permute-done.2
  16.0 1.2 %collective-permute-start.3 = (f32[168,128]{1,0:T(8,128)S(1)}, f32[168,128]{1,0:T(8,128)S(1)}, u32[]{:S(2)}, u32[]{:S(2)}) collective-permute-start(f32[168,128]{1,0:T(8,128)S(1)} %add.32), channel_id=1, source_target_pairs={{0,5},{1,7},{2,4},{3,6},{4,2},{5,0},{6,3},{7,1},{8,14},{9,12},{10,... | collective-permute-start | bytes 258056 | tf_op jit(solution)/shard_map/ppermute | solution.py:262
  17.2 0.9 %collective-permute-done.8 = f32[160,128]{1,0:T(8,128)S(1)} collective-permute-done((f32[160,128]{1,0:T(8,128)S(1)}, f32[160,128]{1,0:T(8,128)S(1)}, u32[]{:S(2)}, u32[]{:S(2)}) %collective-permute-start.8) | collective-permute-done | bytes 81952 | tf_op jit(solution)/shard_map/ppermute | solution.py:262
  18.1 2.0 %collective-permute-start.9 = (f32[160,128]{1,0:T(8,128)S(1)}, f32[160,128]{1,0:T(8,128)S(1)}, u32[]{:S(2)}, u32[]{:S(2)}) collective-permute-start(f32[160,128]{1,0:T(8,128)S(1)} %add.37), channel_id=1, source_target_pairs={{0,12},{1,21},{2,22},{3,15},{4,16},{5,9},{6,10},{7,19},{8,28},{9,5... | collective-permute-start | bytes 245768 | tf_op jit(solution)/shard_map/ppermute | solution.py:262
  20.1 0.0 collective-permute-done.3
  20.1 2.8 %collective-permute-start.4 = (f32[168,128]{1,0:T(8,128)S(1)}, f32[168,128]{1,0:T(8,128)S(1)}, u32[]{:S(2)}, u32[]{:S(2)}) collective-permute-start(f32[168,128]{1,0:T(8,128)S(1)} %add.33), channel_id=1, source_target_pairs={{0,6},{1,4},{2,7},{3,5},{4,1},{5,3},{6,0},{7,2},{8,13},{9,15},{10,... | collective-permute-start | bytes 258056 | tf_op jit(solution)/shard_map/ppermute | solution.py:262
  22.9 0.0 collective-permute-done.9
  22.9 1.2 %collective-permute-start.10 = (f32[160,128]{1,0:T(8,128)S(1)}, f32[160,128]{1,0:T(8,128)S(1)}, u32[]{:S(2)}, u32[]{:S(2)}) collective-permute-start(f32[160,128]{1,0:T(8,128)S(1)} %add.38), channel_id=1, source_target_pairs={{0,20},{1,13},{2,14},{3,23},{4,8},{5,17},{6,18},{7,11},{8,4},{9,29... | collective-permute-start | bytes 245768 | tf_op jit(solution)/shard_map/ppermute | solution.py:262
  24.1 1.2 %collective-permute-done.4 = f32[168,128]{1,0:T(8,128)S(1)} collective-permute-done((f32[168,128]{1,0:T(8,128)S(1)}, f32[168,128]{1,0:T(8,128)S(1)}, u32[]{:S(2)}, u32[]{:S(2)}) %collective-permute-start.4) | collective-permute-done | bytes 86048 | tf_op jit(solution)/shard_map/ppermute | solution.py:262
  25.4 0.8 %collective-permute-start.5 = (f32[168,128]{1,0:T(8,128)S(1)}, f32[168,128]{1,0:T(8,128)S(1)}, u32[]{:S(2)}, u32[]{:S(2)}) collective-permute-start(f32[168,128]{1,0:T(8,128)S(1)} %add.34.refs_0_), channel_id=1, source_target_pairs={{0,4},{4,0},{8,12},{12,8},{16,20},{20,16},{24,28},{28,24},{1,5},{5... | collective-permute-start | bytes 258056 | tf_op jit(solution)/shard_map/ppermute | solution.py:265
  26.2 0.7 %collective-permute-done.10 = f32[160,128]{1,0:T(8,128)S(1)} collective-permute-done((f32[160,128]{1,0:T(8,128)S(1)}, f32[160,128]{1,0:T(8,128)S(1)}, u32[]{:S(2)}, u32[]{:S(2)}) %collective-permute-start.10) | collective-permute-done | bytes 81952 | tf_op jit(solution)/shard_map/ppermute | solution.py:262
  26.9 0.3 %collective-permute-start.11 = (f32[160,128]{1,0:T(8,128)S(1)}, f32[160,128]{1,0:T(8,128)S(1)}, u32[]{:S(2)}, u32[]{:S(2)}) collective-permute-start(f32[160,128]{1,0:T(8,128)S(1)} %add.39.refs_2_), channel_id=1, source_target_pairs={{0,4},{4,0},{8,12},{12,8},{16,20},{20,16},{24,28},{28,24},{1,5},{5... | collective-permute-start | bytes 245768 | tf_op jit(solution)/shard_map/ppermute | solution.py:265
  27.2 1.0 %collective-permute-done.11.refs_3_ = f32[160,128]{1,0:T(8,128)S(1)} collective-permute-done((f32[160,128]{1,0:T(8,128)S(1)}, f32[160,128]{1,0:T(8,128)S(1)}, u32[]{:S(2)}, u32[]{:S(2)}) %collective-permute-start.11) | collective-permute-done | bytes 81952 | tf_op jit(solution)/shard_map/ppermute | solution.py:265
  28.2 0.0 collective-permute-done.5.refs_1_
  28.2 0.8 %shard_map.56 = f32[5,128,128]{2,1,0:T(8,128)} custom-call(f32[168,128]{1,0:T(8,128)S(1)} %add.34.refs_0_, f32[168,128]{1,0:T(8,128)S(1)} %collective-permute-done.5.refs_1_, f32[160,128]{1,0:T(8,128)S(1)} %add.39.refs_2_, f32[160,128]{1,0:T(8,128)S(1)} %collective-permute-done.11.refs_3_), custom_call_target="tpu_custom_call" | custom-call | tf_op jit(solution)/shard_map/pallas_call | solution.py:222
  (10 shorter events, 0.1 us)
Async XLA Ops:
  4.7 1.5 %collective-permute-start = (f32[168,128]{1,0:T(8,128)S(1)}, f32[168,128]{1,0:T(8,128)S(1)}, u32[]{:S(2)}, u32[]{:S(2)}) collective-permute-start(f32[168,128]{1,0:T(8,128)S(1)} %get-tuple-element.10), channel_id=1, source_target_pairs={{0,4},{4,0},{8,12},{12,8},{16,20},{20,16},{24,28},{28,24},{1,5},{5... | collective-permute-start | bytes 258056 | tf_op jit(solution)/shard_map/ppermute | solution.py:258
  5.2 3.6 %collective-permute-start.6 = (f32[160,128]{1,0:T(8,128)S(1)}, f32[160,128]{1,0:T(8,128)S(1)}, u32[]{:S(2)}, u32[]{:S(2)}) collective-permute-start(f32[160,128]{1,0:T(8,128)S(1)} %get-tuple-element.12), channel_id=1, source_target_pairs={{0,4},{4,0},{8,12},{12,8},{16,20},{20,16},{24,28},{28,24},{1,5},{5... | collective-permute-start | bytes 245768 | tf_op jit(solution)/shard_map/ppermute | solution.py:258
  6.2 4.8 %collective-permute-start.1 = (f32[168,128]{1,0:T(8,128)S(1)}, f32[168,128]{1,0:T(8,128)S(1)}, u32[]{:S(2)}, u32[]{:S(2)}) collective-permute-start(f32[168,128]{1,0:T(8,128)S(1)} %add.30), channel_id=1, source_target_pairs={{0,12},{1,21},{2,22},{3,15},{4,16},{5,9},{6,10},{7,19},{8,28},{9,5... | collective-permute-start | bytes 258056 | tf_op jit(solution)/shard_map/ppermute | solution.py:262
  8.8 4.3 %collective-permute-start.7 = (f32[160,128]{1,0:T(8,128)S(1)}, f32[160,128]{1,0:T(8,128)S(1)}, u32[]{:S(2)}, u32[]{:S(2)}) collective-permute-start(f32[160,128]{1,0:T(8,128)S(1)} %add.35), channel_id=1, source_target_pairs={{0,5},{1,7},{2,4},{3,6},{4,2},{5,0},{6,3},{7,1},{8,14},{9,12},{10,... | collective-permute-start | bytes 245768 | tf_op jit(solution)/shard_map/ppermute | solution.py:262
  11.0 4.9 %collective-permute-start.2 = (f32[168,128]{1,0:T(8,128)S(1)}, f32[168,128]{1,0:T(8,128)S(1)}, u32[]{:S(2)}, u32[]{:S(2)}) collective-permute-start(f32[168,128]{1,0:T(8,128)S(1)} %add.31), channel_id=1, source_target_pairs={{0,20},{1,13},{2,14},{3,23},{4,8},{5,17},{6,18},{7,11},{8,4},{9,29... | collective-permute-start | bytes 258056 | tf_op jit(solution)/shard_map/ppermute | solution.py:262
  13.1 4.9 %collective-permute-start.8 = (f32[160,128]{1,0:T(8,128)S(1)}, f32[160,128]{1,0:T(8,128)S(1)}, u32[]{:S(2)}, u32[]{:S(2)}) collective-permute-start(f32[160,128]{1,0:T(8,128)S(1)} %add.36), channel_id=1, source_target_pairs={{0,6},{1,4},{2,7},{3,5},{4,1},{5,3},{6,0},{7,2},{8,13},{9,15},{10,... | collective-permute-start | bytes 245768 | tf_op jit(solution)/shard_map/ppermute | solution.py:262
  16.0 4.1 %collective-permute-start.3 = (f32[168,128]{1,0:T(8,128)S(1)}, f32[168,128]{1,0:T(8,128)S(1)}, u32[]{:S(2)}, u32[]{:S(2)}) collective-permute-start(f32[168,128]{1,0:T(8,128)S(1)} %add.32), channel_id=1, source_target_pairs={{0,5},{1,7},{2,4},{3,6},{4,2},{5,0},{6,3},{7,1},{8,14},{9,12},{10,... | collective-permute-start | bytes 258056 | tf_op jit(solution)/shard_map/ppermute | solution.py:262
  18.1 4.8 %collective-permute-start.9 = (f32[160,128]{1,0:T(8,128)S(1)}, f32[160,128]{1,0:T(8,128)S(1)}, u32[]{:S(2)}, u32[]{:S(2)}) collective-permute-start(f32[160,128]{1,0:T(8,128)S(1)} %add.37), channel_id=1, source_target_pairs={{0,12},{1,21},{2,22},{3,15},{4,16},{5,9},{6,10},{7,19},{8,28},{9,5... | collective-permute-start | bytes 245768 | tf_op jit(solution)/shard_map/ppermute | solution.py:262
  20.1 5.2 %collective-permute-start.4 = (f32[168,128]{1,0:T(8,128)S(1)}, f32[168,128]{1,0:T(8,128)S(1)}, u32[]{:S(2)}, u32[]{:S(2)}) collective-permute-start(f32[168,128]{1,0:T(8,128)S(1)} %add.33), channel_id=1, source_target_pairs={{0,6},{1,4},{2,7},{3,5},{4,1},{5,3},{6,0},{7,2},{8,13},{9,15},{10,... | collective-permute-start | bytes 258056 | tf_op jit(solution)/shard_map/ppermute | solution.py:262
  22.9 3.9 %collective-permute-start.10 = (f32[160,128]{1,0:T(8,128)S(1)}, f32[160,128]{1,0:T(8,128)S(1)}, u32[]{:S(2)}, u32[]{:S(2)}) collective-permute-start(f32[160,128]{1,0:T(8,128)S(1)} %add.38), channel_id=1, source_target_pairs={{0,20},{1,13},{2,14},{3,23},{4,8},{5,17},{6,18},{7,11},{8,4},{9,29... | collective-permute-start | bytes 245768 | tf_op jit(solution)/shard_map/ppermute | solution.py:262
  25.4 2.9 %collective-permute-start.5 = (f32[168,128]{1,0:T(8,128)S(1)}, f32[168,128]{1,0:T(8,128)S(1)}, u32[]{:S(2)}, u32[]{:S(2)}) collective-permute-start(f32[168,128]{1,0:T(8,128)S(1)} %add.34.refs_0_), channel_id=1, source_target_pairs={{0,4},{4,0},{8,12},{12,8},{16,20},{20,16},{24,28},{28,24},{1,5},{5... | collective-permute-start | bytes 258056 | tf_op jit(solution)/shard_map/ppermute | solution.py:265
  26.9 1.3 %collective-permute-start.11 = (f32[160,128]{1,0:T(8,128)S(1)}, f32[160,128]{1,0:T(8,128)S(1)}, u32[]{:S(2)}, u32[]{:S(2)}) collective-permute-start(f32[160,128]{1,0:T(8,128)S(1)} %add.39.refs_2_), channel_id=1, source_target_pairs={{0,4},{4,0},{8,12},{12,8},{16,20},{20,16},{24,28},{28,24},{1,5},{5... | collective-permute-start | bytes 245768 | tf_op jit(solution)/shard_map/ppermute | solution.py:265

commit v6 on v4

--- a/solution.py
+++ b/solution.py
@@ -1,3 +1,4 @@
+import functools
 import math
 
 import jax
@@ -186,20 +187,24 @@
     return (k // 2) * ROWS + (half ^ (k % 2)) * HALF
 
 
-def finish(*refs):
-    *parts, psf_ref = refs
-    squares = parts[0][TERMS * HALF :, :]
+def finish(stream, *refs):
+    first_ref, mine_ref, away_ref = refs[0], refs[-5], refs[-4]
+    psf_hbm, rows_ref, sent = refs[-3:]
+    squares = first_ref[TERMS * HALF :, :]
     scale = 1.0 / jnp.sqrt(jnp.sum(jnp.sum(squares, axis=1, keepdims=True), axis=0, keepdims=True))
 
     def put(half):
-        for k, ref in enumerate(parts):
-            first = first_row(k, half)
+        for k, ref in enumerate((mine_ref, away_ref)):
+            first = (half ^ k) * HALF
             for term in range(TERMS):
-                psf_ref[term, first : first + HALF, :] = ref[term * HALF : (term + 1) * HALF, :] * scale
+                rows_ref[term, first : first + HALF, :] = ref[term * HALF : (term + 1) * HALF, :] * scale
 
     half = half_of(lax.axis_index("chan"), lax.axis_index("space"))
     pl.when(half == 0)(lambda: put(0))
     pl.when(half == 1)(lambda: put(1))
+    copy = pltpu.make_async_copy(rows_ref, psf_hbm.at[:, stream * ROWS : (stream + 1) * ROWS, :], sent)
+    copy.start()
+    copy.wait()
 
 
 VMEM = pl.BlockSpec(memory_space=pltpu.VMEM)
@@ -232,13 +237,19 @@
 
 
 def whole_patch(parts):
-    return pl.pallas_call(
-        finish,
-        out_shape=jax.ShapeDtypeStruct((TERMS, P_SIZE, P_SIZE), jnp.float32),
-        in_specs=[VMEM] * len(parts),
-        out_specs=VMEM,
-        compiler_params=pltpu.CompilerParams(vmem_limit_bytes=4 << 20),
-    )(*parts)
+    psf = None
+    for stream in range(STREAMS):
+        args = [parts[0]] + ([] if psf is None else [psf]) + parts[2 * stream : 2 * stream + 2]
+        psf = pl.pallas_call(
+            functools.partial(finish, stream),
+            out_shape=jax.ShapeDtypeStruct((TERMS, P_SIZE, P_SIZE), jnp.float32),
+            in_specs=[VMEM] + ([] if psf is None else [HBM]) + [VMEM, VMEM],
+            out_specs=HBM,
+            input_output_aliases={} if psf is None else {1: 0},
+            scratch_shapes=[pltpu.VMEM((TERMS, ROWS, P_SIZE), jnp.float32), pltpu.SemaphoreType.DMA],
+            compiler_params=pltpu.CompilerParams(vmem_limit_bytes=4 << 20),
+        )(*args)
+    return psf
 
 
 def exchange_orders(chan, space):

time: 28.7 us -> 28.6 us (level)
  waiting for transfers between devices: 5.22 us -> 4.43 us
  Pallas kernels: 4.98 us -> 5.7 us
    ppermute x2, waiting for transfers between devices: 1.06 us -> 0.26 us  [on_device(): parts += [total, lax.ppermute(total, 'chan', partner)]]
    pallas_call x1 -> x2, Pallas kernels: 0.84 us -> 1.57 us  [whole_patch(): pl.pallas_call(functools.partial(finish, stream), out_shape=jax.ShapeDtyp...]
  transfers between devices with their start and end apart: 12 -> 12, of which waited for: 6 -> 6; matrix products, arithmetic and copies ran while one was open for 0% -> 0% of each run, Pallas kernels for 0% -> 3%
where the time goes in v6:
time: 28.6 us; the launch traced here: 28.5 us
  starting transfers between devices  18.2 us (64%)
  Pallas kernels  5.7 us (20%)
  waiting for transfers between devices  4.43 us (15%)
    ppermute x8, starting transfers between devices, on_device(): lax.ppermute(totals[k], ('chan', 'space'), pairs_of(moves, chan, space))  16.4 us
    pallas_call x1, Pallas kernels, partial_beams(): pl.pallas_call(kernel, out_shape=(part_a, part_a, part_b, part_b), in_spe...  4.13 us
    ppermute x8, waiting for transfers between devices, on_device(): lax.ppermute(totals[k], ('chan', 'space'), pairs_of(moves, chan, space))  3.31 us
    pallas_call x2, Pallas kernels, whole_patch(): pl.pallas_call(functools.partial(finish, stream), out_shape=jax.ShapeDtyp...  1.57 us
    ppermute x2, starting transfers between devices, on_device(): parts += [total, lax.ppermute(total, 'chan', partner)]  1.13 us
    ppermute x2, waiting for transfers between devices, on_device(): lax.ppermute(other, 'chan', partner)  0.85 us
    ppermute x2, starting transfers between devices, on_device(): lax.ppermute(other, 'chan', partner)  0.63 us
  transfers between devices with their start and end apart: 12, of which 6 were waited for; matrix products, arithmetic and copies ran while one was open for 0% of the time, Pallas kernels for 3%

profile of v6, /device:TPU:0, one launch (start us, length us, event | category | flops | bytes accessed | tf_op | source)
XLA Modules:
  0.0 28.5 jit_solution(17085561596099914264)
XLA Ops:
  0.0 4.1 %shard_map.55 = (f32[168,128]{1,0:T(8,128)S(1)}, f32[168,128]{1,0:T(8,128)S(1)}, f32[160,128]{1,0:T(8,128)S(1)}, f32[160,128]{1,0:T(8,128)S(1)}) custom-call(s32[2]{0:T(128)} %crop_hbm.1, f32[8]{0:T(128)} %tau_hbm.1, s32[8,2048]{1,0:T(8,128)} %u_hbm.1, s32[8,2048]{1,0:T(8,128)} %v_hbm.1, f32[8,2048]{1,0:T(8,128)} %w_hbm.1), custom_call_target="tpu_custom_call" | custom-call | tf_op jit(solution)/shard_map/pallas_call | solution.py:217
  4.1 0.6 %collective-permute-start = (f32[168,128]{1,0:T(8,128)S(1)}, f32[168,128]{1,0:T(8,128)S(1)}, u32[]{:S(2)}, u32[]{:S(2)}) collective-permute-start(f32[168,128]{1,0:T(8,128)S(1)} %get-tuple-element.10), channel_id=1, source_target_pairs={{0,4},{4,0},{8,12},{12,8},{16,20},{20,16},{24,28},{28,24},{1,5},{5... | collective-permute-start | bytes 258056 | tf_op jit(solution)/shard_map/ppermute | solution.py:282
  4.7 0.1 collective-permute-start.6
  4.8 0.8 %collective-permute-done = f32[168,128]{1,0:T(8,128)S(1)} collective-permute-done((f32[168,128]{1,0:T(8,128)S(1)}, f32[168,128]{1,0:T(8,128)S(1)}, u32[]{:S(2)}, u32[]{:S(2)}) %collective-permute-start) | collective-permute-done | bytes 86048 | tf_op jit(solution)/shard_map/ppermute | solution.py:282
  5.6 2.7 %collective-permute-start.1 = (f32[168,128]{1,0:T(8,128)S(1)}, f32[168,128]{1,0:T(8,128)S(1)}, u32[]{:S(2)}, u32[]{:S(2)}) collective-permute-start(f32[168,128]{1,0:T(8,128)S(1)} %add.30), channel_id=1, source_target_pairs={{0,12},{1,21},{2,22},{3,15},{4,16},{5,9},{6,10},{7,19},{8,28},{9,5... | collective-permute-start | bytes 258056 | tf_op jit(solution)/shard_map/ppermute | solution.py:286
  8.3 0.0 collective-permute-done.6
  8.3 1.6 %collective-permute-start.7 = (f32[160,128]{1,0:T(8,128)S(1)}, f32[160,128]{1,0:T(8,128)S(1)}, u32[]{:S(2)}, u32[]{:S(2)}) collective-permute-start(f32[160,128]{1,0:T(8,128)S(1)} %add.35), channel_id=1, source_target_pairs={{0,5},{1,7},{2,4},{3,6},{4,2},{5,0},{6,3},{7,1},{8,14},{9,12},{10,... | collective-permute-start | bytes 245768 | tf_op jit(solution)/shard_map/ppermute | solution.py:286
  9.9 0.6 %collective-permute-done.1 = f32[168,128]{1,0:T(8,128)S(1)} collective-permute-done((f32[168,128]{1,0:T(8,128)S(1)}, f32[168,128]{1,0:T(8,128)S(1)}, u32[]{:S(2)}, u32[]{:S(2)}) %collective-permute-start.1) | collective-permute-done | bytes 86048 | tf_op jit(solution)/shard_map/ppermute | solution.py:286
  10.5 2.1 %collective-permute-start.2 = (f32[168,128]{1,0:T(8,128)S(1)}, f32[168,128]{1,0:T(8,128)S(1)}, u32[]{:S(2)}, u32[]{:S(2)}) collective-permute-start(f32[168,128]{1,0:T(8,128)S(1)} %add.31), channel_id=1, source_target_pairs={{0,20},{1,13},{2,14},{3,23},{4,8},{5,17},{6,18},{7,11},{8,4},{9,29... | collective-permute-start | bytes 258056 | tf_op jit(solution)/shard_map/ppermute | solution.py:286
  12.6 0.0 collective-permute-done.7
  12.6 2.8 %collective-permute-start.8 = (f32[160,128]{1,0:T(8,128)S(1)}, f32[160,128]{1,0:T(8,128)S(1)}, u32[]{:S(2)}, u32[]{:S(2)}) collective-permute-start(f32[160,128]{1,0:T(8,128)S(1)} %add.36), channel_id=1, source_target_pairs={{0,6},{1,4},{2,7},{3,5},{4,1},{5,3},{6,0},{7,2},{8,13},{9,15},{10,... | collective-permute-start | bytes 245768 | tf_op jit(solution)/shard_map/ppermute | solution.py:286
  15.4 0.0 collective-permute-done.2
  15.4 1.2 %collective-permute-start.3 = (f32[168,128]{1,0:T(8,128)S(1)}, f32[168,128]{1,0:T(8,128)S(1)}, u32[]{:S(2)}, u32[]{:S(2)}) collective-permute-start(f32[168,128]{1,0:T(8,128)S(1)} %add.32), channel_id=1, source_target_pairs={{0,5},{1,7},{2,4},{3,6},{4,2},{5,0},{6,3},{7,1},{8,14},{9,12},{10,... | collective-permute-start | bytes 258056 | tf_op jit(solution)/shard_map/ppermute | solution.py:286
  16.7 0.9 %collective-permute-done.8 = f32[160,128]{1,0:T(8,128)S(1)} collective-permute-done((f32[160,128]{1,0:T(8,128)S(1)}, f32[160,128]{1,0:T(8,128)S(1)}, u32[]{:S(2)}, u32[]{:S(2)}) %collective-permute-start.8) | collective-permute-done | bytes 81952 | tf_op jit(solution)/shard_map/ppermute | solution.py:286
  17.6 2.0 %collective-permute-start.9 = (f32[160,128]{1,0:T(8,128)S(1)}, f32[160,128]{1,0:T(8,128)S(1)}, u32[]{:S(2)}, u32[]{:S(2)}) collective-permute-start(f32[160,128]{1,0:T(8,128)S(1)} %add.37), channel_id=1, source_target_pairs={{0,12},{1,21},{2,22},{3,15},{4,16},{5,9},{6,10},{7,19},{8,28},{9,5... | collective-permute-start | bytes 245768 | tf_op jit(solution)/shard_map/ppermute | solution.py:286
  19.6 0.0 collective-permute-done.3
  19.6 2.8 %collective-permute-start.4 = (f32[168,128]{1,0:T(8,128)S(1)}, f32[168,128]{1,0:T(8,128)S(1)}, u32[]{:S(2)}, u32[]{:S(2)}) collective-permute-start(f32[168,128]{1,0:T(8,128)S(1)} %add.33), channel_id=1, source_target_pairs={{0,6},{1,4},{2,7},{3,5},{4,1},{5,3},{6,0},{7,2},{8,13},{9,15},{10,... | collective-permute-start | bytes 258056 | tf_op jit(solution)/shard_map/ppermute | solution.py:286
  22.4 0.0 collective-permute-done.9
  22.4 1.2 %collective-permute-start.10 = (f32[160,128]{1,0:T(8,128)S(1)}, f32[160,128]{1,0:T(8,128)S(1)}, u32[]{:S(2)}, u32[]{:S(2)}) collective-permute-start(f32[160,128]{1,0:T(8,128)S(1)} %add.38), channel_id=1, source_target_pairs={{0,20},{1,13},{2,14},{3,23},{4,8},{5,17},{6,18},{7,11},{8,4},{9,29... | collective-permute-start | bytes 245768 | tf_op jit(solution)/shard_map/ppermute | solution.py:286
  23.6 1.2 %collective-permute-done.4 = f32[168,128]{1,0:T(8,128)S(1)} collective-permute-done((f32[168,128]{1,0:T(8,128)S(1)}, f32[168,128]{1,0:T(8,128)S(1)}, u32[]{:S(2)}, u32[]{:S(2)}) %collective-permute-start.4) | collective-permute-done | bytes 86048 | tf_op jit(solution)/shard_map/ppermute | solution.py:286
  24.8 0.8 %collective-permute-start.5 = (f32[168,128]{1,0:T(8,128)S(1)}, f32[168,128]{1,0:T(8,128)S(1)}, u32[]{:S(2)}, u32[]{:S(2)}) collective-permute-start(f32[168,128]{1,0:T(8,128)S(1)} %add.34.refs_0_.refs_1_), channel_id=1, source_target_pairs={{0,4},{4,0},{8,12},{12,8},{16,20},{20,16},{24,28},{28,24},{1,5},{5... | collective-permute-start | bytes 258056 | tf_op jit(solution)/shard_map/ppermute | solution.py:289
  25.7 0.7 %collective-permute-done.10 = f32[160,128]{1,0:T(8,128)S(1)} collective-permute-done((f32[160,128]{1,0:T(8,128)S(1)}, f32[160,128]{1,0:T(8,128)S(1)}, u32[]{:S(2)}, u32[]{:S(2)}) %collective-permute-start.10) | collective-permute-done | bytes 81952 | tf_op jit(solution)/shard_map/ppermute | solution.py:286
  26.3 0.3 %collective-permute-start.11 = (f32[160,128]{1,0:T(8,128)S(1)}, f32[160,128]{1,0:T(8,128)S(1)}, u32[]{:S(2)}, u32[]{:S(2)}) collective-permute-start(f32[160,128]{1,0:T(8,128)S(1)} %add.39.refs_2_), channel_id=1, source_target_pairs={{0,4},{4,0},{8,12},{12,8},{16,20},{20,16},{24,28},{28,24},{1,5},{5... | collective-permute-start | bytes 245768 | tf_op jit(solution)/shard_map/ppermute | solution.py:289
  26.6 0.0 collective-permute-done.5.refs_2_
  26.6 0.8 %shard_map.56.refs_1_ = f32[5,128,128]{2,1,0:T(8,128)} custom-call(f32[168,128]{1,0:T(8,128)S(1)} %add.34.refs_0_.refs_1_, f32[168,128]{1,0:T(8,128)S(1)} %add.34.refs_0_.refs_1_, f32[168,128]{1,0:T(8,128)S(1)} %collective-permute-done.5.refs_2_), custom_call_target="tpu_custom_call" | custom-call | tf_op jit(solution)/shard_map/pallas_call | solution.py:243
  27.4 0.3 collective-permute-done.11.refs_3_
  27.7 0.8 %shard_map.57 = f32[5,128,128]{2,1,0:T(8,128)} custom-call(f32[168,128]{1,0:T(8,128)S(1)} %add.34.refs_0_.refs_1_, f32[5,128,128]{2,1,0:T(8,128)} %shard_map.56.refs_1_, f32[160,128]{1,0:T(8,128)S(1)} %add.39.refs_2_, f32[160,128]{1,0:T(8,128)S(1)} %collective-permute-done.11.refs_3_), custom_call_target="tpu_custom_call", output_to_operand_aliasing={{}: (1, {})} | custom-call | tf_op jit(solution)/shard_map/pallas_call | solution.py:243
  (10 shorter events, 0.1 us)
Async XLA Ops:
  4.1 1.5 %collective-permute-start = (f32[168,128]{1,0:T(8,128)S(1)}, f32[168,128]{1,0:T(8,128)S(1)}, u32[]{:S(2)}, u32[]{:S(2)}) collective-permute-start(f32[168,128]{1,0:T(8,128)S(1)} %get-tuple-element.10), channel_id=1, source_target_pairs={{0,4},{4,0},{8,12},{12,8},{16,20},{20,16},{24,28},{28,24},{1,5},{5... | collective-permute-start | bytes 258056 | tf_op jit(solution)/shard_map/ppermute | solution.py:282
  4.7 3.6 %collective-permute-start.6 = (f32[160,128]{1,0:T(8,128)S(1)}, f32[160,128]{1,0:T(8,128)S(1)}, u32[]{:S(2)}, u32[]{:S(2)}) collective-permute-start(f32[160,128]{1,0:T(8,128)S(1)} %get-tuple-element.12), channel_id=1, source_target_pairs={{0,4},{4,0},{8,12},{12,8},{16,20},{20,16},{24,28},{28,24},{1,5},{5... | collective-permute-start | bytes 245768 | tf_op jit(solution)/shard_map/ppermute | solution.py:282
  5.6 4.8 %collective-permute-start.1 = (f32[168,128]{1,0:T(8,128)S(1)}, f32[168,128]{1,0:T(8,128)S(1)}, u32[]{:S(2)}, u32[]{:S(2)}) collective-permute-start(f32[168,128]{1,0:T(8,128)S(1)} %add.30), channel_id=1, source_target_pairs={{0,12},{1,21},{2,22},{3,15},{4,16},{5,9},{6,10},{7,19},{8,28},{9,5... | collective-permute-start | bytes 258056 | tf_op jit(solution)/shard_map/ppermute | solution.py:286
  8.3 4.3 %collective-permute-start.7 = (f32[160,128]{1,0:T(8,128)S(1)}, f32[160,128]{1,0:T(8,128)S(1)}, u32[]{:S(2)}, u32[]{:S(2)}) collective-permute-start(f32[160,128]{1,0:T(8,128)S(1)} %add.35), channel_id=1, source_target_pairs={{0,5},{1,7},{2,4},{3,6},{4,2},{5,0},{6,3},{7,1},{8,14},{9,12},{10,... | collective-permute-start | bytes 245768 | tf_op jit(solution)/shard_map/ppermute | solution.py:286
  10.5 4.9 %collective-permute-start.2 = (f32[168,128]{1,0:T(8,128)S(1)}, f32[168,128]{1,0:T(8,128)S(1)}, u32[]{:S(2)}, u32[]{:S(2)}) collective-permute-start(f32[168,128]{1,0:T(8,128)S(1)} %add.31), channel_id=1, source_target_pairs={{0,20},{1,13},{2,14},{3,23},{4,8},{5,17},{6,18},{7,11},{8,4},{9,29... | collective-permute-start | bytes 258056 | tf_op jit(solution)/shard_map/ppermute | solution.py:286
  12.6 4.9 %collective-permute-start.8 = (f32[160,128]{1,0:T(8,128)S(1)}, f32[160,128]{1,0:T(8,128)S(1)}, u32[]{:S(2)}, u32[]{:S(2)}) collective-permute-start(f32[160,128]{1,0:T(8,128)S(1)} %add.36), channel_id=1, source_target_pairs={{0,6},{1,4},{2,7},{3,5},{4,1},{5,3},{6,0},{7,2},{8,13},{9,15},{10,... | collective-permute-start | bytes 245768 | tf_op jit(solution)/shard_map/ppermute | solution.py:286
  15.4 4.1 %collective-permute-start.3 = (f32[168,128]{1,0:T(8,128)S(1)}, f32[168,128]{1,0:T(8,128)S(1)}, u32[]{:S(2)}, u32[]{:S(2)}) collective-permute-start(f32[168,128]{1,0:T(8,128)S(1)} %add.32), channel_id=1, source_target_pairs={{0,5},{1,7},{2,4},{3,6},{4,2},{5,0},{6,3},{7,1},{8,14},{9,12},{10,... | collective-permute-start | bytes 258056 | tf_op jit(solution)/shard_map/ppermute | solution.py:286
  17.6 4.8 %collective-permute-start.9 = (f32[160,128]{1,0:T(8,128)S(1)}, f32[160,128]{1,0:T(8,128)S(1)}, u32[]{:S(2)}, u32[]{:S(2)}) collective-permute-start(f32[160,128]{1,0:T(8,128)S(1)} %add.37), channel_id=1, source_target_pairs={{0,12},{1,21},{2,22},{3,15},{4,16},{5,9},{6,10},{7,19},{8,28},{9,5... | collective-permute-start | bytes 245768 | tf_op jit(solution)/shard_map/ppermute | solution.py:286
  19.6 5.2 %collective-permute-start.4 = (f32[168,128]{1,0:T(8,128)S(1)}, f32[168,128]{1,0:T(8,128)S(1)}, u32[]{:S(2)}, u32[]{:S(2)}) collective-permute-start(f32[168,128]{1,0:T(8,128)S(1)} %add.33), channel_id=1, source_target_pairs={{0,6},{1,4},{2,7},{3,5},{4,1},{5,3},{6,0},{7,2},{8,13},{9,15},{10,... | collective-permute-start | bytes 258056 | tf_op jit(solution)/shard_map/ppermute | solution.py:286
  22.4 3.9 %collective-permute-start.10 = (f32[160,128]{1,0:T(8,128)S(1)}, f32[160,128]{1,0:T(8,128)S(1)}, u32[]{:S(2)}, u32[]{:S(2)}) collective-permute-start(f32[160,128]{1,0:T(8,128)S(1)} %add.38), channel_id=1, source_target_pairs={{0,20},{1,13},{2,14},{3,23},{4,8},{5,17},{6,18},{7,11},{8,4},{9,29... | collective-permute-start | bytes 245768 | tf_op jit(solution)/shard_map/ppermute | solution.py:286
  24.8 1.8 %collective-permute-start.5 = (f32[168,128]{1,0:T(8,128)S(1)}, f32[168,128]{1,0:T(8,128)S(1)}, u32[]{:S(2)}, u32[]{:S(2)}) collective-permute-start(f32[168,128]{1,0:T(8,128)S(1)} %add.34.refs_0_.refs_1_), channel_id=1, source_target_pairs={{0,4},{4,0},{8,12},{12,8},{16,20},{20,16},{24,28},{28,24},{1,5},{5... | collective-permute-start | bytes 258056 | tf_op jit(solution)/shard_map/ppermute | solution.py:289
  26.3 1.3 %collective-permute-start.11 = (f32[160,128]{1,0:T(8,128)S(1)}, f32[160,128]{1,0:T(8,128)S(1)}, u32[]{:S(2)}, u32[]{:S(2)}) collective-permute-start(f32[160,128]{1,0:T(8,128)S(1)} %add.39.refs_2_), channel_id=1, source_target_pairs={{0,4},{4,0},{8,12},{12,8},{16,20},{20,16},{24,28},{28,24},{1,5},{5... | collective-permute-start | bytes 245768 | tf_op jit(solution)/shard_map/ppermute | solution.py:289

commit v7 on v6

--- a/solution.py
+++ b/solution.py
@@ -255,13 +255,12 @@
 def exchange_orders(chan, space):
     over_chan = [("chan", 1 << b) for b in range(1, chan.bit_length() - 1)]
     over_space = [("space", 1 << b) for b in range(space.bit_length() - 1)]
-    orders = []
-    for order in (over_chan + over_space, over_space + over_chan):
-        swapped = list(order)
-        for k in range(0, len(order) - 1, 2):
-            swapped[k], swapped[k + 1] = order[k + 1], order[k]
-        orders.append(list(zip(order, swapped)))
-    return orders
+    middle = len(over_space) // 2
+    order = over_space[:middle] + over_chan + over_space[middle:]
+    swapped = list(order)
+    for k in range(0, len(order) - 1, 2):
+        swapped[k], swapped[k + 1] = order[k + 1], order[k]
+    return [list(zip(order, swapped)), list(zip(swapped[::-1], order[::-1]))]
 
 
 def pairs_of(moves, chan, space):

time: 28.6 us -> 28.5 us (level)
  starting transfers between devices: 18.2 us -> 17.7 us
    ppermute x2, starting transfers between devices: 1.13 us -> 0.4 us  [on_device(): parts += [total, lax.ppermute(total, 'chan', partner)]]
  transfers between devices with their start and end apart: 12 -> 12, of which waited for: 6 -> 7; matrix products, arithmetic and copies ran while one was open for 0% -> 0% of each run, Pallas kernels for 3% -> 3%
where the time goes in v7:
time: 28.5 us; the launch traced here: 28.1 us
  starting transfers between devices  17.7 us (62%)
  Pallas kernels  5.7 us (20%)
  waiting for transfers between devices  4.63 us (16%)
    ppermute x8, starting transfers between devices, on_device(): lax.ppermute(totals[k], ('chan', 'space'), pairs_of(moves, chan, space))  16.6 us
    pallas_call x1, Pallas kernels, partial_beams(): pl.pallas_call(kernel, out_shape=(part_a, part_a, part_b, part_b), in_spe...  4.13 us
    ppermute x8, waiting for transfers between devices, on_device(): lax.ppermute(totals[k], ('chan', 'space'), pairs_of(moves, chan, space))  3.52 us
    pallas_call x2, Pallas kernels, whole_patch(): pl.pallas_call(functools.partial(finish, stream), out_shape=jax.ShapeDtyp...  1.57 us
    ppermute x2, waiting for transfers between devices, on_device(): lax.ppermute(other, 'chan', partner)  0.85 us
    ppermute x2, starting transfers between devices, on_device(): lax.ppermute(other, 'chan', partner)  0.63 us
  transfers between devices with their start and end apart: 12, of which 7 were waited for; matrix products, arithmetic and copies ran while one was open for 0% of the time, Pallas kernels for 3%

profile of v7, /device:TPU:0, one launch (start us, length us, event | category | flops | bytes accessed | tf_op | source)
XLA Modules:
  0.0 28.1 jit_solution(16321497453852640602)
XLA Ops:
  0.0 4.1 %shard_map.55 = (f32[168,128]{1,0:T(8,128)S(1)}, f32[168,128]{1,0:T(8,128)S(1)}, f32[160,128]{1,0:T(8,128)S(1)}, f32[160,128]{1,0:T(8,128)S(1)}) custom-call(s32[2]{0:T(128)} %crop_hbm.1, f32[8]{0:T(128)} %tau_hbm.1, s32[8,2048]{1,0:T(8,128)} %u_hbm.1, s32[8,2048]{1,0:T(8,128)} %v_hbm.1, f32[8,2048]{1,0:T(8,128)} %w_hbm.1), custom_call_target="tpu_custom_call" | custom-call | tf_op jit(solution)/shard_map/pallas_call | solution.py:217
  4.1 0.6 %collective-permute-start = (f32[168,128]{1,0:T(8,128)S(1)}, f32[168,128]{1,0:T(8,128)S(1)}, u32[]{:S(2)}, u32[]{:S(2)}) collective-permute-start(f32[168,128]{1,0:T(8,128)S(1)} %get-tuple-element.10), channel_id=1, source_target_pairs={{0,4},{4,0},{8,12},{12,8},{16,20},{20,16},{24,28},{28,24},{1,5},{5... | collective-permute-start | bytes 258056 | tf_op jit(solution)/shard_map/ppermute | solution.py:281
  4.7 0.1 collective-permute-start.6
  4.8 0.8 %collective-permute-done = f32[168,128]{1,0:T(8,128)S(1)} collective-permute-done((f32[168,128]{1,0:T(8,128)S(1)}, f32[168,128]{1,0:T(8,128)S(1)}, u32[]{:S(2)}, u32[]{:S(2)}) %collective-permute-start) | collective-permute-done | bytes 86048 | tf_op jit(solution)/shard_map/ppermute | solution.py:281
  5.6 2.7 %collective-permute-start.1 = (f32[168,128]{1,0:T(8,128)S(1)}, f32[168,128]{1,0:T(8,128)S(1)}, u32[]{:S(2)}, u32[]{:S(2)}) collective-permute-start(f32[168,128]{1,0:T(8,128)S(1)} %add.30), channel_id=1, source_target_pairs={{0,5},{1,13},{2,14},{3,6},{4,8},{5,0},{6,3},{7,11},{8,4},{9,12},{1... | collective-permute-start | bytes 258056 | tf_op jit(solution)/shard_map/ppermute | solution.py:285
  8.4 0.0 collective-permute-done.6
  8.4 1.5 %collective-permute-start.7 = (f32[160,128]{1,0:T(8,128)S(1)}, f32[160,128]{1,0:T(8,128)S(1)}, u32[]{:S(2)}, u32[]{:S(2)}) collective-permute-start(f32[160,128]{1,0:T(8,128)S(1)} %add.35), channel_id=1, source_target_pairs={{0,20},{1,7},{2,4},{3,23},{4,2},{5,17},{6,18},{7,1},{8,14},{9,29},... | collective-permute-start | bytes 245768 | tf_op jit(solution)/shard_map/ppermute | solution.py:285
  9.9 0.6 %collective-permute-done.1 = f32[168,128]{1,0:T(8,128)S(1)} collective-permute-done((f32[168,128]{1,0:T(8,128)S(1)}, f32[168,128]{1,0:T(8,128)S(1)}, u32[]{:S(2)}, u32[]{:S(2)}) %collective-permute-start.1) | collective-permute-done | bytes 86048 | tf_op jit(solution)/shard_map/ppermute | solution.py:285
  10.6 2.0 %collective-permute-start.2 = (f32[168,128]{1,0:T(8,128)S(1)}, f32[168,128]{1,0:T(8,128)S(1)}, u32[]{:S(2)}, u32[]{:S(2)}) collective-permute-start(f32[168,128]{1,0:T(8,128)S(1)} %add.31), channel_id=1, source_target_pairs={{0,12},{1,4},{2,7},{3,15},{4,1},{5,9},{6,10},{7,2},{8,13},{9,5},{1... | collective-permute-start | bytes 258056 | tf_op jit(solution)/shard_map/ppermute | solution.py:285
  12.6 0.0 collective-permute-done.7
  12.6 2.6 %collective-permute-start.8 = (f32[160,128]{1,0:T(8,128)S(1)}, f32[160,128]{1,0:T(8,128)S(1)}, u32[]{:S(2)}, u32[]{:S(2)}) collective-permute-start(f32[160,128]{1,0:T(8,128)S(1)} %add.36), channel_id=1, source_target_pairs={{0,6},{1,21},{2,22},{3,5},{4,16},{5,3},{6,0},{7,19},{8,28},{9,15},... | collective-permute-start | bytes 245768 | tf_op jit(solution)/shard_map/ppermute | solution.py:285
  15.3 0.0 collective-permute-done.2
  15.3 2.1 %collective-permute-start.3 = (f32[168,128]{1,0:T(8,128)S(1)}, f32[168,128]{1,0:T(8,128)S(1)}, u32[]{:S(2)}, u32[]{:S(2)}) collective-permute-start(f32[168,128]{1,0:T(8,128)S(1)} %add.32), channel_id=1, source_target_pairs={{0,20},{1,7},{2,4},{3,23},{4,2},{5,17},{6,18},{7,1},{8,14},{9,29},... | collective-permute-start | bytes 258056 | tf_op jit(solution)/shard_map/ppermute | solution.py:285
  17.4 0.1 collective-permute-done.8
  17.5 1.3 %collective-permute-start.9 = (f32[160,128]{1,0:T(8,128)S(1)}, f32[160,128]{1,0:T(8,128)S(1)}, u32[]{:S(2)}, u32[]{:S(2)}) collective-permute-start(f32[160,128]{1,0:T(8,128)S(1)} %add.37), channel_id=1, source_target_pairs={{0,5},{1,13},{2,14},{3,6},{4,8},{5,0},{6,3},{7,11},{8,4},{9,12},{1... | collective-permute-start | bytes 245768 | tf_op jit(solution)/shard_map/ppermute | solution.py:285
  18.8 0.8 %collective-permute-done.3 = f32[168,128]{1,0:T(8,128)S(1)} collective-permute-done((f32[168,128]{1,0:T(8,128)S(1)}, f32[168,128]{1,0:T(8,128)S(1)}, u32[]{:S(2)}, u32[]{:S(2)}) %collective-permute-start.3) | collective-permute-done | bytes 86048 | tf_op jit(solution)/shard_map/ppermute | solution.py:285
  19.6 2.5 %collective-permute-start.4 = (f32[168,128]{1,0:T(8,128)S(1)}, f32[168,128]{1,0:T(8,128)S(1)}, u32[]{:S(2)}, u32[]{:S(2)}) collective-permute-start(f32[168,128]{1,0:T(8,128)S(1)} %add.33), channel_id=1, source_target_pairs={{0,6},{1,21},{2,22},{3,5},{4,16},{5,3},{6,0},{7,19},{8,28},{9,15},... | collective-permute-start | bytes 258056 | tf_op jit(solution)/shard_map/ppermute | solution.py:285
  22.1 0.0 collective-permute-done.9
  22.1 1.8 %collective-permute-start.10 = (f32[160,128]{1,0:T(8,128)S(1)}, f32[160,128]{1,0:T(8,128)S(1)}, u32[]{:S(2)}, u32[]{:S(2)}) collective-permute-start(f32[160,128]{1,0:T(8,128)S(1)} %add.38), channel_id=1, source_target_pairs={{0,12},{1,4},{2,7},{3,15},{4,1},{5,9},{6,10},{7,2},{8,13},{9,5},{1... | collective-permute-start | bytes 245768 | tf_op jit(solution)/shard_map/ppermute | solution.py:285
  23.8 0.6 %collective-permute-done.4 = f32[168,128]{1,0:T(8,128)S(1)} collective-permute-done((f32[168,128]{1,0:T(8,128)S(1)}, f32[168,128]{1,0:T(8,128)S(1)}, u32[]{:S(2)}, u32[]{:S(2)}) %collective-permute-start.4) | collective-permute-done | bytes 86048 | tf_op jit(solution)/shard_map/ppermute | solution.py:285
  24.5 0.1 collective-permute-start.5
  24.6 1.4 %collective-permute-done.10 = f32[160,128]{1,0:T(8,128)S(1)} collective-permute-done((f32[160,128]{1,0:T(8,128)S(1)}, f32[160,128]{1,0:T(8,128)S(1)}, u32[]{:S(2)}, u32[]{:S(2)}) %collective-permute-start.10) | collective-permute-done | bytes 81952 | tf_op jit(solution)/shard_map/ppermute | solution.py:285
  26.0 0.3 %collective-permute-start.11 = (f32[160,128]{1,0:T(8,128)S(1)}, f32[160,128]{1,0:T(8,128)S(1)}, u32[]{:S(2)}, u32[]{:S(2)}) collective-permute-start(f32[160,128]{1,0:T(8,128)S(1)} %add.39.refs_2_), channel_id=1, source_target_pairs={{0,4},{4,0},{8,12},{12,8},{16,20},{20,16},{24,28},{28,24},{1,5},{5... | collective-permute-start | bytes 245768 | tf_op jit(solution)/shard_map/ppermute | solution.py:288
  26.3 0.0 collective-permute-done.5.refs_2_
  26.3 0.8 %shard_map.56.refs_1_ = f32[5,128,128]{2,1,0:T(8,128)} custom-call(f32[168,128]{1,0:T(8,128)S(1)} %add.34.refs_0_.refs_1_, f32[168,128]{1,0:T(8,128)S(1)} %add.34.refs_0_.refs_1_, f32[168,128]{1,0:T(8,128)S(1)} %collective-permute-done.5.refs_2_), custom_call_target="tpu_custom_call" | custom-call | tf_op jit(solution)/shard_map/pallas_call | solution.py:243
  27.1 0.3 collective-permute-done.11.refs_3_
  27.4 0.8 %shard_map.57 = f32[5,128,128]{2,1,0:T(8,128)} custom-call(f32[168,128]{1,0:T(8,128)S(1)} %add.34.refs_0_.refs_1_, f32[5,128,128]{2,1,0:T(8,128)} %shard_map.56.refs_1_, f32[160,128]{1,0:T(8,128)S(1)} %add.39.refs_2_, f32[160,128]{1,0:T(8,128)S(1)} %collective-permute-done.11.refs_3_), custom_call_target="tpu_custom_call", output_to_operand_aliasing={{}: (1, {})} | custom-call | tf_op jit(solution)/shard_map/pallas_call | solution.py:243
  (10 shorter events, 0.1 us)
Async XLA Ops:
  4.1 1.5 %collective-permute-start = (f32[168,128]{1,0:T(8,128)S(1)}, f32[168,128]{1,0:T(8,128)S(1)}, u32[]{:S(2)}, u32[]{:S(2)}) collective-permute-start(f32[168,128]{1,0:T(8,128)S(1)} %get-tuple-element.10), channel_id=1, source_target_pairs={{0,4},{4,0},{8,12},{12,8},{16,20},{20,16},{24,28},{28,24},{1,5},{5... | collective-permute-start | bytes 258056 | tf_op jit(solution)/shard_map/ppermute | solution.py:281
  4.7 3.7 %collective-permute-start.6 = (f32[160,128]{1,0:T(8,128)S(1)}, f32[160,128]{1,0:T(8,128)S(1)}, u32[]{:S(2)}, u32[]{:S(2)}) collective-permute-start(f32[160,128]{1,0:T(8,128)S(1)} %get-tuple-element.12), channel_id=1, source_target_pairs={{0,4},{4,0},{8,12},{12,8},{16,20},{20,16},{24,28},{28,24},{1,5},{5... | collective-permute-start | bytes 245768 | tf_op jit(solution)/shard_map/ppermute | solution.py:281
  5.6 4.9 %collective-permute-start.1 = (f32[168,128]{1,0:T(8,128)S(1)}, f32[168,128]{1,0:T(8,128)S(1)}, u32[]{:S(2)}, u32[]{:S(2)}) collective-permute-start(f32[168,128]{1,0:T(8,128)S(1)} %add.30), channel_id=1, source_target_pairs={{0,5},{1,13},{2,14},{3,6},{4,8},{5,0},{6,3},{7,11},{8,4},{9,12},{1... | collective-permute-start | bytes 258056 | tf_op jit(solution)/shard_map/ppermute | solution.py:285
  8.4 4.2 %collective-permute-start.7 = (f32[160,128]{1,0:T(8,128)S(1)}, f32[160,128]{1,0:T(8,128)S(1)}, u32[]{:S(2)}, u32[]{:S(2)}) collective-permute-start(f32[160,128]{1,0:T(8,128)S(1)} %add.35), channel_id=1, source_target_pairs={{0,20},{1,7},{2,4},{3,23},{4,2},{5,17},{6,18},{7,1},{8,14},{9,29},... | collective-permute-start | bytes 245768 | tf_op jit(solution)/shard_map/ppermute | solution.py:285
  10.6 4.7 %collective-permute-start.2 = (f32[168,128]{1,0:T(8,128)S(1)}, f32[168,128]{1,0:T(8,128)S(1)}, u32[]{:S(2)}, u32[]{:S(2)}) collective-permute-start(f32[168,128]{1,0:T(8,128)S(1)} %add.31), channel_id=1, source_target_pairs={{0,12},{1,4},{2,7},{3,15},{4,1},{5,9},{6,10},{7,2},{8,13},{9,5},{1... | collective-permute-start | bytes 258056 | tf_op jit(solution)/shard_map/ppermute | solution.py:285
  12.6 4.8 %collective-permute-start.8 = (f32[160,128]{1,0:T(8,128)S(1)}, f32[160,128]{1,0:T(8,128)S(1)}, u32[]{:S(2)}, u32[]{:S(2)}) collective-permute-start(f32[160,128]{1,0:T(8,128)S(1)} %add.36), channel_id=1, source_target_pairs={{0,6},{1,21},{2,22},{3,5},{4,16},{5,3},{6,0},{7,19},{8,28},{9,15},... | collective-permute-start | bytes 245768 | tf_op jit(solution)/shard_map/ppermute | solution.py:285
  15.3 4.3 %collective-permute-start.3 = (f32[168,128]{1,0:T(8,128)S(1)}, f32[168,128]{1,0:T(8,128)S(1)}, u32[]{:S(2)}, u32[]{:S(2)}) collective-permute-start(f32[168,128]{1,0:T(8,128)S(1)} %add.32), channel_id=1, source_target_pairs={{0,20},{1,7},{2,4},{3,23},{4,2},{5,17},{6,18},{7,1},{8,14},{9,29},... | collective-permute-start | bytes 258056 | tf_op jit(solution)/shard_map/ppermute | solution.py:285
  17.5 4.6 %collective-permute-start.9 = (f32[160,128]{1,0:T(8,128)S(1)}, f32[160,128]{1,0:T(8,128)S(1)}, u32[]{:S(2)}, u32[]{:S(2)}) collective-permute-start(f32[160,128]{1,0:T(8,128)S(1)} %add.37), channel_id=1, source_target_pairs={{0,5},{1,13},{2,14},{3,6},{4,8},{5,0},{6,3},{7,11},{8,4},{9,12},{1... | collective-permute-start | bytes 245768 | tf_op jit(solution)/shard_map/ppermute | solution.py:285
  19.6 4.9 %collective-permute-start.4 = (f32[168,128]{1,0:T(8,128)S(1)}, f32[168,128]{1,0:T(8,128)S(1)}, u32[]{:S(2)}, u32[]{:S(2)}) collective-permute-start(f32[168,128]{1,0:T(8,128)S(1)} %add.33), channel_id=1, source_target_pairs={{0,6},{1,21},{2,22},{3,5},{4,16},{5,3},{6,0},{7,19},{8,28},{9,15},... | collective-permute-start | bytes 258056 | tf_op jit(solution)/shard_map/ppermute | solution.py:285
  22.1 3.9 %collective-permute-start.10 = (f32[160,128]{1,0:T(8,128)S(1)}, f32[160,128]{1,0:T(8,128)S(1)}, u32[]{:S(2)}, u32[]{:S(2)}) collective-permute-start(f32[160,128]{1,0:T(8,128)S(1)} %add.38), channel_id=1, source_target_pairs={{0,12},{1,4},{2,7},{3,15},{4,1},{5,9},{6,10},{7,2},{8,13},{9,5},{1... | collective-permute-start | bytes 245768 | tf_op jit(solution)/shard_map/ppermute | solution.py:285
  24.5 1.9 %collective-permute-start.5 = (f32[168,128]{1,0:T(8,128)S(1)}, f32[168,128]{1,0:T(8,128)S(1)}, u32[]{:S(2)}, u32[]{:S(2)}) collective-permute-start(f32[168,128]{1,0:T(8,128)S(1)} %add.34.refs_0_.refs_1_), channel_id=1, source_target_pairs={{0,4},{4,0},{8,12},{12,8},{16,20},{20,16},{24,28},{28,24},{1,5},{5... | collective-permute-start | bytes 258056 | tf_op jit(solution)/shard_map/ppermute | solution.py:288
  26.0 1.3 %collective-permute-start.11 = (f32[160,128]{1,0:T(8,128)S(1)}, f32[160,128]{1,0:T(8,128)S(1)}, u32[]{:S(2)}, u32[]{:S(2)}) collective-permute-start(f32[160,128]{1,0:T(8,128)S(1)} %add.39.refs_2_), channel_id=1, source_target_pairs={{0,4},{4,0},{8,12},{12,8},{16,20},{20,16},{24,28},{28,24},{1,5},{5... | collective-permute-start | bytes 245768 | tf_op jit(solution)/shard_map/ppermute | solution.py:288
